TPU v7x, 256 devices: a whole 4x4x8 slice. The times are simulated.
256 devices in a mesh: atom: 128 (over z, y, x), chan: 2 (over core).
Axes of the slice: x: 4, y: 4, z: 8, core: 2. Of those that a mesh axis runs over, the one named last changes fastest.
Arguments:
- features: bfloat16 [128, 49, 32768], P('chan', None, 'atom'), may hold values from -6 to 6
- weights: bfloat16 [3, 7, 128, 128], P(None, None, None, 'chan'), may hold values from -2 to 2
- cotangent: bfloat16 [128, 49, 32768], P('chan', None, 'atom'), may hold values from -6 to 6
- edge_bias: float32 [8, 16, 32768], P('chan', None, 'atom'), may hold values from -5 to 5
- neighbours: int32 [16, 32768], P(None, 'atom'), may hold values from 0 to 32767, as said below
- valid_mask: int32 [16, 32768], P(None, 'atom'), may hold values from 0 to 1, as said below
Outputs:
- grad_features: bfloat16 [128, 49, 32768], P('chan', None, 'atom')
- grad_weights: float32 [3, 7, 128, 128], P(None, None, None, 'chan')
- grad_bias: float32 [8, 16, 32768], P('chan', None, 'atom')
Inputs may be any that keep to these rules, and one draw needn't show every extreme that they name: neighbours[s, a] = (a + o) mod 32768 with -128 <= o <= 128; offsets of -128 and 128 both occur, and slot 0 always holds (a - 1) mod 32768. `valid_mask`: slot 0 of every atom is valid; the share of valid slots rises along the atom order from about a quarter to nearly all.
All inputs are finite; a program needn't handle non-finite values.
Results may differ from a plain program's by a relative error of at most 0.005.
The roundings to bfloat16 on the way count: a program that leaves them out, or rounds other values in their place, can miss the bound.
Values may be sent and summed in bfloat16 or wider, within the bound.
A program may use at most 128 MiB of HBM per device.

v0:
```python
import math

import jax
import jax.numpy as jnp
from jax import lax
from jax.sharding import Mesh
from jax.sharding import PartitionSpec as P

LMAX = 6
HALO = 128
ATOM = ("atom_0", "atom_1", "atom_2")


soft_cap = 10.0
highest = lax.Precision.HIGHEST


def extended_2(cells, sides, width):
    for axis, dim in sides:
        count = lax.axis_size(axis)
        head = lax.slice_in_dim(cells, 0, width, axis=dim)
        tail = lax.slice_in_dim(cells, cells.shape[dim] - width, cells.shape[dim], axis=dim)
        cells = jnp.concatenate(
            [
                lax.ppermute(tail, axis, [(i, (i + 1) % count) for i in range(count)]),
                cells,
                lax.ppermute(head, axis, [((i + 1) % count, i) for i in range(count)]),
            ],
            axis=dim,
        )
    return cells


def cut_along(x, dim, count):
    before, after = (x.shape[:dim], x.shape[dim + 1 :])
    return jnp.moveaxis(x.reshape(*before, count, -1, *after), dim, 0)


def summed_on_arrival(x, axis, dim):
    tiles = cut_along(x, dim, lax.axis_size(axis))
    arrived = lax.all_to_all(tiles, axis, split_axis=0, concat_axis=0, tiled=True)
    return arrived.sum(axis=0)


def sum_in_two_steps(x, axes, dim):
    far, near = axes
    tiles = cut_along(x, dim, lax.axis_size(far))
    nearer = summed_on_arrival(tiles, near, dim + 1)
    arrived = lax.all_to_all(nearer, far, split_axis=0, concat_axis=0, tiled=True)
    return arrived.sum(axis=0)


def rows_for(lines, count):
    spare = -lines.shape[0] % count
    if not spare:
        return lines
    return jnp.concatenate([lines, jnp.zeros((spare, *lines.shape[1:]), lines.dtype)])


def from_everyone(x, axis):
    count = lax.axis_size(axis)
    return lax.all_to_all(jnp.broadcast_to(x[None], (count, *x.shape)), axis, 0, 0, tiled=True)


def in_order(tiles, dim):
    shape = list(tiles.shape[1:])
    shape[dim] *= tiles.shape[0]
    return jnp.moveaxis(tiles, 0, dim).reshape(shape)


def whole_of(x, axes, dim):
    far, near = axes
    leading = from_everyone(x, far)
    tiles = jnp.swapaxes(from_everyone(leading, near), 0, 1)
    return in_order(tiles.reshape(-1, *x.shape), dim)


def total_of(x, axes):
    lines = x.reshape(-1, x.shape[-1])
    own = sum_in_two_steps(
        rows_for(lines, lax.axis_size(axes[0]) * lax.axis_size(axes[1])), axes, 0
    )
    whole = whole_of(own, axes, 0)
    return whole[: len(lines)].reshape(x.shape)


def degree_bounds():
    return [(degree * degree, (degree + 1) * (degree + 1)) for degree in range(LMAX + 1)]


def on_device(features, weights, cotangent, edge_bias, neighbours, valid_mask):
    chan_local = features.shape[0]
    comps = features.shape[1]
    atoms_dev = features.shape[2]
    heads_local = edge_bias.shape[0]
    head_rows = chan_local // heads_local * comps
    score_scale = 1.0 / math.sqrt(head_rows)
    total_atoms = atoms_dev * lax.axis_size(ATOM)
    extended = atoms_dev + 2 * HALO
    gathered = lax.all_gather(features, "chan", axis=0, tiled=True)
    projected = jnp.concatenate(
        [
            jnp.einsum(
                "cma,gcd->gdma",
                gathered[:, low_comp:high_comp],
                weights[:, degree],
                preferred_element_type=jnp.float32,
            )
            for degree, (low_comp, high_comp) in enumerate(degree_bounds())
        ],
        axis=2,
    ).astype(jnp.bfloat16)
    keyval = extended_2(projected[1:3], ((ATOM, 3),), HALO)
    keyval = keyval.reshape(2, heads_local, head_rows, extended)
    query_all = projected[0].reshape(heads_local, head_rows, atoms_dev)
    grad_out = cotangent.reshape(heads_local, head_rows, atoms_dev)
    first_atom = lax.axis_index(ATOM) * atoms_dev
    local_index = (neighbours - first_atom + HALO) % total_atoms
    slot_table = jnp.where(
        local_index[:, None, :] == jnp.arange(extended, dtype=jnp.int32)[None, :, None],
        jnp.float32(1.0),
        jnp.float32(0.0),
    )
    live_slots = valid_mask > 0
    query_grads = []
    scatter_list = []
    logit_grads = []
    for head in range(heads_local):
        query_h = query_all[head]
        grad_h = grad_out[head]
        keys_h = keyval[0, head]
        values_h = keyval[1, head]
        query_keys = jnp.einsum("fa,fj->aj", query_h, keys_h, preferred_element_type=jnp.float32)
        grad_values = jnp.einsum("fa,fj->aj", grad_h, values_h, preferred_element_type=jnp.float32)
        raw_score = score_scale * jnp.einsum(
            "aj,sja->sa", query_keys, slot_table, precision=highest
        )
        squashed = jnp.tanh(raw_score / soft_cap)
        logits = soft_cap * squashed + edge_bias[head]
        exp_logit = jnp.where(live_slots, jnp.exp(logits), jnp.float32(0.0))
        attention = exp_logit / jnp.sum(exp_logit, axis=0, keepdims=True)
        grad_attn = jnp.einsum("aj,sja->sa", grad_values, slot_table, precision=highest)
        grad_logit = attention * (grad_attn - jnp.sum(attention * grad_attn, axis=0, keepdims=True))
        grad_raw = score_scale * grad_logit * (1.0 - squashed * squashed)
        raw_spread = jnp.einsum("sa,sja->ja", grad_raw, slot_table, precision=highest)
        attn_spread = jnp.einsum("sa,sja->ja", attention, slot_table, precision=highest)
        grad_query = jnp.einsum(
            "fj,ja->fa", keys_h.astype(jnp.float32), raw_spread, precision=highest
        )
        key_sums = jnp.einsum(
            "fa,ja->fj", query_h.astype(jnp.float32), raw_spread, precision=highest
        )
        value_sums = jnp.einsum(
            "fa,ja->fj", grad_h.astype(jnp.float32), attn_spread, precision=highest
        )
        query_grads.append(grad_query)
        scatter_list.append(jnp.stack([key_sums, value_sums]))
        logit_grads.append(grad_logit)
    sums_all = jnp.stack(scatter_list, axis=1)
    own_rows = sums_all[..., HALO : HALO + atoms_dev]
    left_rim = sums_all[..., :HALO]
    right_rim = sums_all[..., HALO + atoms_dev :]
    edge_rims = extended_2(jnp.concatenate([left_rim, right_rim], axis=3), ((ATOM, 3),), HALO)
    from_prev = edge_rims[..., :HALO]
    from_next = edge_rims[..., edge_rims.shape[3] - HALO :]
    own_rows = own_rows.at[..., :HALO].add(from_prev)
    own_rows = own_rows.at[..., atoms_dev - HALO :].add(from_next)
    grads = jnp.stack([jnp.stack(query_grads), own_rows[0], own_rows[1]]).astype(jnp.bfloat16)
    grads = grads.reshape(3, chan_local, comps, atoms_dev)
    weight_terms = jnp.stack(
        [
            jnp.einsum(
                "cma,gdma->gcd",
                gathered[:, low_comp:high_comp],
                grads[:, :, low_comp:high_comp],
                preferred_element_type=jnp.float32,
            )
            for low_comp, high_comp in degree_bounds()
        ],
        axis=1,
    )
    grad_weights = total_of(weight_terms, (("atom_0", "atom_1"), "atom_2"))
    grad_features = summed_on_arrival(
        jnp.concatenate(
            [
                jnp.einsum(
                    "gcd,gdma->cma",
                    weights[:, degree],
                    grads[:, :, low_comp:high_comp],
                    preferred_element_type=jnp.float32,
                )
                for degree, (low_comp, high_comp) in enumerate(degree_bounds())
            ],
            axis=1,
        ),
        "chan",
        0,
    )
    return (grad_features.astype(jnp.bfloat16), grad_weights, jnp.stack(logit_grads))


def solution(mesh):
    split = Mesh(
        mesh.devices.reshape(8, 4, 4, mesh.shape["chan"]), ("atom_0", "atom_1", "atom_2", "chan")
    )
    placed = (
        P("chan", None, ATOM),
        P(None, None, None, "chan"),
        P("chan", None, ATOM),
        P("chan", None, ATOM),
        P(None, ATOM),
        P(None, ATOM),
    )
    return jax.shard_map(
        on_device,
        mesh=split,
        in_specs=placed,
        out_specs=(P("chan", None, ATOM), P(None, None, None, "chan"), P("chan", None, ATOM)),
        check_vma=False,
    )
```

profile of v0, /device:TPU:1, one launch (start us, length us, event | category | flops | bytes accessed | tf_op | source)
XLA Modules:
  0.0 368.4 jit_solution(1511911419688474568)
XLA Ops:
  7.9 24.0 %all-gather.2.cloned.1.call-done = bf16[128,49,256]{2,0,1:T(8,128)(2,1)} async-done(((bf16[64,49,256]{2,0,1:T(8,128)(2,1)}), bf16[128,49,256]{2,0,1:T(8,128)(2,1)}) %all-gather.2.cloned.1.call-update) | async-done | bytes 3211280 | tf_op jit(solution)/shard_map/all_gather | solution.py:100
  44.5 7.1 %collective-permute-start.1 = (bf16[2,64,49,128]{3,1,2,0:T(8,128)(2,1)}, bf16[2,64,49,128]{3,1,2,0:T(8,128)(2,1)}, u32[]{:S(2)}, u32[]{:S(2)}) collective-permute-start(bf16[2,64,49,128]{3,1,2,0:T(8,128)(2,1)} %get-tuple-element.86), channel_id=1, source_target_pairs={{2,0},{4,2},{6,4},{8,6},{10,8},{12,10},{14,12},{16,14},{18,16},{20... | collective-permute-start | bytes 4816904 | tf_op jit(solution)/shard_map/ppermute | solution.py:27
  74.5 11.6 %collective-permute-done.1 = bf16[2,64,49,128]{3,1,2,0:T(8,128)(2,1)} collective-permute-done((bf16[2,64,49,128]{3,1,2,0:T(8,128)(2,1)}, bf16[2,64,49,128]{3,1,2,0:T(8,128)(2,1)}, u32[]{:S(2)}, u32[]{:S(2)}) %collective-permute-start.1) | collective-permute-done | bytes 1605664 | tf_op jit(solution)/shard_map/ppermute | solution.py:27
  86.1 7.3 %collective-permute-done = bf16[2,64,49,128]{3,1,2,0:T(8,128)(2,1)} collective-permute-done((bf16[2,64,49,128]{3,1,2,0:T(8,128)(2,1)}, bf16[2,64,49,128]{3,1,2,0:T(8,128)(2,1)}, u32[]{:S(2)}, u32[]{:S(2)}) %collective-permute-start) | collective-permute-done | bytes 1605664 | tf_op jit(solution)/shard_map/ppermute | solution.py:25
  93.5 3.7 pad_maximum_fusion.1
  97.2 26.7 %copy.145 = bf16[2,64,49,512]{3,0,2,1:T(2,128)(2,1)S(1)} copy(bf16[2,64,49,512]{3,1,2,0:T(8,128)(2,1)S(1)} %pad_maximum_fusion.1) | data formatting | bytes 12845056 | tf_op jit(solution)/shard_map/concatenate | solution.py:23
  123.9 10.0 %fusion.170 = (bf16[1,1,784,512]{3,0,2,1:T(2,128)(2,1)S(1)}, bf16[1,1,784,512]{3,0,2,1:T(2,128)(2,1)S(1)}, bf16[1,1,784,512]{3,0,2,1:T(2,128)(2,1)S(1)}, bf16[1,...) fusion(bf16[2,4,784,512]{3,0,2,1:T(2,128)(2,1)S(1)} %bitcast.597), kind=kLoop, calls=%fused_computation.252 | loop fusion | bytes 12845056 | tf_op jit(solution)/shard_map/slice | solution.py:131
  138.1 8.8 %fusion.25 = (f32[256,16]{0,1:T(8,128)S(1)}, f32[256,16]{0,1:T(8,128)S(1)}, f32[256,16]{0,1:T(8,128)S(1)}, f32[256,16]{0,1:T(8,128)S(1)}, f32[256,16]{0,1:T(8,12...) fusion(f32[256,512]{0,1:T(8,128)S(1)} %convolution_bitcast_fusion.11, ...), kind=kLoop, calls=%fused_computation.28 | loop fusion | flops 37715968 | bytes 4341760 | tf_op jit(solution)/shard_map/aj,sja->sa/dot_general | solution.py:142
  148.2 6.7 %fusion.20 = (f32[256,512]{0,1:T(8,128)S(1)}, f32[256,512]{0,1:T(8,128)S(1)}, f32[256,512]{0,1:T(8,128)S(1)}, f32[256,512]{0,1:T(8,128)S(1)}, f32[256,512]{0,1:T...) fusion(f32[256,16]{0,1:T(8,128)S(1)} %bitcast.611, ...), kind=kLoop, calls=%fused_computation.23 | loop fusion | flops 36700160 | bytes 4341760 | tf_op jit(solution)/shard_map/sa,sja->ja/dot_general | solution.py:146
  164.7 3.4 fusion.169
  168.1 7.1 %collective-permute-start.3 = (f32[2,4,784,128]{3,2,0,1:T(8,128)}, f32[2,4,784,128]{3,2,0,1:T(8,128)}, u32[]{:S(2)}, u32[]{:S(2)}) collective-permute-start(f32[2,4,784,128]{3,2,0,1:T(8,128)} %get-tuple-element.71), channel_id=1, source_target_pairs={{2,0},{4,2},{6,4},{8,6},{10,8},{12,10},{14,12},{16,14},{18,16},{20... | collective-permute-start | bytes 9633800 | tf_op jit(solution)/shard_map/ppermute | solution.py:27
  183.3 60.3 %collective-permute-done.2 = f32[2,4,784,128]{3,2,0,1:T(8,128)} collective-permute-done((f32[2,4,784,128]{3,2,0,1:T(8,128)}, f32[2,4,784,128]{3,2,0,1:T(8,128)}, u32[]{:S(2)}, u32[]{:S(2)}) %collective-permute-start.2) | collective-permute-done | bytes 3211296 | tf_op jit(solution)/shard_map/ppermute | solution.py:25
  243.6 4.9 %fusion.33 = f32[2,4,784,256]{3,2,0,1:T(8,128)} fusion(f32[2,4,784,256]{3,2,0,1:T(8,128)} %slice.310, f32[2,4,784,128]{3,2,0,1:T(8,128)} %collective-permute-done.2, f32[2,4,784,512]{3,2,0,1:T(8,128)} %copy-done), kind=kLoop, calls=%fused_computation.40 | loop fusion | flops 802816 | bytes 9633792 | tf_op jit(solution)/shard_map/scatter-add | solution.py:166
  248.5 4.9 %fusion.32 = f32[2,4,784,256]{3,2,0,1:T(8,128)} fusion(f32[2,4,784,256]{3,2,0,1:T(8,128)} %fusion.33, f32[2,4,784,128]{3,2,0,1:T(8,128)} %collective-permute-done.3), kind=kLoop, calls=%fused_computation.38 | loop fusion | flops 802816 | bytes 9633792 | tf_op jit(solution)/shard_map/scatter-add | solution.py:167
  270.5 3.9 %all-to-all-start.1 = ((f32[4,1,43008]{2,1,0:T(1,128)}), f32[4,1,43008]{2,1,0:T(1,128)S(1)}, u32[]{:S(2)}, u32[]{:S(2)}) async-start(f32[4,1,43008]{2,1,0:T(1,128)} %reshape.194), calls=%async_computation.1 | async-start | bytes 1376256 | tf_op jit(solution)/shard_map/all_to_all | solution.py:41
  283.7 3.5 reduce.36
  290.3 4.3 %all-to-all-start.2 = ((f32[32,1,1344]{2,1,0:T(1,128)}), f32[32,1,1344]{2,1,0:T(1,128)S(1)}, u32[]{:S(2)}, u32[]{:S(2)}) async-start(f32[32,1,1344]{2,1,0:T(1,128)} %reshape.196), calls=%async_computation.2 | async-start | bytes 360448 | tf_op jit(solution)/shard_map/all_to_all | solution.py:49
  298.7 5.6 %all-to-all-done.2 = f32[32,1,1344]{2,1,0:T(1,128)S(1)} async-done(((f32[32,1,1344]{2,1,0:T(1,128)}), f32[32,1,1344]{2,1,0:T(1,128)S(1)}, u32[]{:S(2)}, u32[]{:S(2)}) %all-to-all-start.2) | async-done | bytes 172064 | tf_op jit(solution)/shard_map/all_to_all | solution.py:49
  309.5 3.9 %all-to-all-start.3 = ((f32[32,1,1344]{2,1,0:T(1,128)}), f32[32,1,1344]{2,1,0:T(1,128)S(1)}, u32[]{:S(2)}, u32[]{:S(2)}) async-start(f32[32,1,1344]{2,1,0:T(1,128)} %reshape.198), calls=%async_computation.3 | async-start | bytes 360448 | tf_op jit(solution)/shard_map/all_to_all | solution.py:62
  316.0 7.2 %all-to-all-done.3 = f32[32,1,1344]{2,1,0:T(1,128)S(1)} async-done(((f32[32,1,1344]{2,1,0:T(1,128)}), f32[32,1,1344]{2,1,0:T(1,128)S(1)}, u32[]{:S(2)}, u32[]{:S(2)}) %all-to-all-start.3) | async-done | bytes 172064 | tf_op jit(solution)/shard_map/all_to_all | solution.py:62
  323.2 12.2 %all-to-all-start = ((f32[2,64,49,256]{3,1,2,0:T(8,128)}), f32[2,64,49,256]{3,1,2,0:T(8,128)}, u32[]{:S(2)}, u32[]{:S(2)}) async-start(f32[2,64,49,256]{3,1,2,0:T(8,128)} %copy_dynamic-update-slice_fusion.1), calls=%async_computation | async-start | bytes 12845056 | tf_op jit(solution)/shard_map/all_to_all | solution.py:41
  341.2 3.7 all-to-all-start.4
  345.5 5.0 %reduce_sum.107 = bf16[64,49,256]{2,0,1:T(8,128)(2,1)} reduce(f32[2,64,49,256]{3,1,2,0:T(8,128)} %all-to-all-done, f32[]{:T(128)} %constant.105.clone.1), dimensions={0}, to_apply=%region_8.9 | reduce | flops 802816 | bytes 8028164 | tf_op jit(solution)/shard_map/reduce_sum | solution.py:42
  350.5 5.2 %all-to-all-done.4 = f32[4,1,43008]{2,1,0:T(1,128)S(1)} async-done(((f32[4,1,43008]{2,1,0:T(1,128)}), f32[4,1,43008]{2,1,0:T(1,128)S(1)}, u32[]{:S(2)}, u32[]{:S(2)}) %all-to-all-start.4) | async-done | bytes 688160 | tf_op jit(solution)/shard_map/all_to_all | solution.py:62
  (162 shorter events, 112.3 us)
Async XLA Ops:
  7.2 28.2 %copy-start.14 = (bf16[3,7,128,64]{2,3,1,0:T(8,128)(2,1)S(1)}, bf16[3,7,128,64]{2,3,1,0:T(8,128)(2,1)}, u32[]{:S(2)}) copy-start(bf16[3,7,128,64]{2,3,1,0:T(8,128)(2,1)} %param.11) | copy-start | bytes 1032196
  7.2 24.7 %all-gather.2.cloned.1.call-start = ((), (), s32[]{:S(2)}) async-start(), calls=%async_computation.5 | async-start | bytes 4816896 | tf_op jit(solution)/shard_map/all_gather | solution.py:100
  41.4 10.2 %copy-start.5 = (bf16[64,49,256]{2,0,1:T(8,128)(2,1)S(1)}, bf16[64,49,256]{2,0,1:T(8,128)(2,1)}, u32[]{:S(2)}) copy-start(bf16[64,49,256]{2,0,1:T(8,128)(2,1)} %param.12) | copy-start | bytes 4816900
  44.5 41.6 %collective-permute-start.1 = (bf16[2,64,49,128]{3,1,2,0:T(8,128)(2,1)}, bf16[2,64,49,128]{3,1,2,0:T(8,128)(2,1)}, u32[]{:S(2)}, u32[]{:S(2)}) collective-permute-start(bf16[2,64,49,128]{3,1,2,0:T(8,128)(2,1)} %get-tuple-element.86), channel_id=1, source_target_pairs={{2,0},{4,2},{6,4},{8,6},{10,8},{12,10},{14,12},{16,14},{18,16},{20... | collective-permute-start | bytes 4816904 | tf_op jit(solution)/shard_map/ppermute | solution.py:27
  51.6 41.9 %collective-permute-start = (bf16[2,64,49,128]{3,1,2,0:T(8,128)(2,1)}, bf16[2,64,49,128]{3,1,2,0:T(8,128)(2,1)}, u32[]{:S(2)}, u32[]{:S(2)}) collective-permute-start(bf16[2,64,49,128]{3,1,2,0:T(8,128)(2,1)} %get-tuple-element.85), channel_id=1, source_target_pairs={{0,2},{2,4},{4,6},{6,8},{8,10},{10,12},{12,14},{14,16},{16,18},{18... | collective-permute-start | bytes 4816904 | tf_op jit(solution)/shard_map/ppermute | solution.py:25
  51.9 4.0 %copy-start.21 = (s32[16,256]{1,0:T(8,128)S(1)}, s32[16,256]{1,0:T(8,128)}, u32[]{:S(2)}) copy-start(s32[16,256]{1,0:T(8,128)} %param.14) | copy-start | bytes 49156
  123.8 10.1 %copy-start.6 = (bf16[784,256]{1,0:T(8,128)(2,1)S(1)}, bf16[784,256]{1,0:T(8,128)(2,1)}, u32[]{:S(2)}) copy-start(bf16[784,256]{1,0:T(8,128)(2,1)} %squeeze.99) | copy-start | bytes 1204228
  123.9 10.6 %copy-start.10 = (bf16[784,256]{1,0:T(8,128)(2,1)S(1)}, bf16[784,256]{1,0:T(8,128)(2,1)}, u32[]{:S(2)}) copy-start(bf16[784,256]{1,0:T(8,128)(2,1)} %squeeze.101) | copy-start | bytes 1204228
  137.5 9.3 %copy-start.16 = (f32[4,16,256]{2,1,0:T(8,128)S(1)}, f32[4,16,256]{2,1,0:T(8,128)}, u32[]{:S(2)}) copy-start(f32[4,16,256]{2,1,0:T(8,128)} %param.13) | copy-start | bytes 196612
  137.6 9.3 %copy-start.20 = (s32[16,256]{1,0:T(8,128)S(1)}, s32[16,256]{1,0:T(8,128)}, u32[]{:S(2)}) copy-start(s32[16,256]{1,0:T(8,128)} %param.15) | copy-start | bytes 49156
  164.7 10.5 %copy-start = (f32[2,4,784,512]{3,2,0,1:T(8,128)}, f32[2,4,784,512]{3,2,0,1:T(8,128)S(1)}, u32[]{:S(2)}) copy-start(f32[2,4,784,512]{3,2,0,1:T(8,128)S(1)} %pad_maximum_fusion) | copy-start | bytes 38535172
  168.1 75.4 %collective-permute-start.2 = (f32[2,4,784,128]{3,2,0,1:T(8,128)}, f32[2,4,784,128]{3,2,0,1:T(8,128)}, u32[]{:S(2)}, u32[]{:S(2)}) collective-permute-start(f32[2,4,784,128]{3,2,0,1:T(8,128)} %get-tuple-element.72), channel_id=1, source_target_pairs={{0,2},{2,4},{4,6},{6,8},{8,10},{10,12},{12,14},{14,16},{16,18},{18... | collective-permute-start | bytes 9633800 | tf_op jit(solution)/shard_map/ppermute | solution.py:25
  168.1 80.3 %collective-permute-start.3 = (f32[2,4,784,128]{3,2,0,1:T(8,128)}, f32[2,4,784,128]{3,2,0,1:T(8,128)}, u32[]{:S(2)}, u32[]{:S(2)}) collective-permute-start(f32[2,4,784,128]{3,2,0,1:T(8,128)} %get-tuple-element.71), channel_id=1, source_target_pairs={{2,0},{4,2},{6,4},{8,6},{10,8},{12,10},{14,12},{16,14},{18,16},{20... | collective-permute-start | bytes 9633800 | tf_op jit(solution)/shard_map/ppermute | solution.py:27
  260.0 6.9 %copy-start.1 = (bf16[3,64,49,256]{3,1,0,2:T(8,128)(2,1)}, bf16[3,64,49,256]{3,1,0,2:T(8,128)(2,1)S(1)}, u32[]{:S(2)}) copy-start(bf16[3,64,49,256]{3,1,0,2:T(8,128)(2,1)S(1)} %copy_dynamic-update-slice_fusion) | copy-start | bytes 14450692
  260.2 4.7 %copy-start.3 = (bf16[128,49,256]{2,0,1:T(8,128)(2,1)S(1)}, bf16[128,49,256]{2,0,1:T(8,128)(2,1)}, u32[]{:S(2)}) copy-start(bf16[128,49,256]{2,0,1:T(8,128)(2,1)} %all-gather.2.cloned.1.call-done) | copy-start | bytes 9633796
  268.7 8.4 %copy-start.4 = (f32[7,256,128,1]{1,2,3,0:T(8,128)S(1)}, f32[7,256,128,1]{1,2,3,0:T(8,128)}, u32[]{:S(2)}) copy-start(f32[7,256,128,1]{1,2,3,0:T(8,128)} %fusion.112) | copy-start | bytes 2752516
  270.5 12.7 %all-to-all-start.1 = ((f32[4,1,43008]{2,1,0:T(1,128)}), f32[4,1,43008]{2,1,0:T(1,128)S(1)}, u32[]{:S(2)}, u32[]{:S(2)}) async-start(f32[4,1,43008]{2,1,0:T(1,128)} %reshape.194), calls=%async_computation.1 | async-start | bytes 1376256 | tf_op jit(solution)/shard_map/all_to_all | solution.py:41
  290.3 14.1 %all-to-all-start.2 = ((f32[32,1,1344]{2,1,0:T(1,128)}), f32[32,1,1344]{2,1,0:T(1,128)S(1)}, u32[]{:S(2)}, u32[]{:S(2)}) async-start(f32[32,1,1344]{2,1,0:T(1,128)} %reshape.196), calls=%async_computation.2 | async-start | bytes 360448 | tf_op jit(solution)/shard_map/all_to_all | solution.py:49
  309.5 13.7 %all-to-all-start.3 = ((f32[32,1,1344]{2,1,0:T(1,128)}), f32[32,1,1344]{2,1,0:T(1,128)S(1)}, u32[]{:S(2)}, u32[]{:S(2)}) async-start(f32[32,1,1344]{2,1,0:T(1,128)} %reshape.198), calls=%async_computation.3 | async-start | bytes 360448 | tf_op jit(solution)/shard_map/all_to_all | solution.py:62
  323.2 18.0 %all-to-all-start = ((f32[2,64,49,256]{3,1,2,0:T(8,128)}), f32[2,64,49,256]{3,1,2,0:T(8,128)}, u32[]{:S(2)}, u32[]{:S(2)}) async-start(f32[2,64,49,256]{3,1,2,0:T(8,128)} %copy_dynamic-update-slice_fusion.1), calls=%async_computation | async-start | bytes 12845056 | tf_op jit(solution)/shard_map/all_to_all | solution.py:41
  336.6 8.3 %copy-start.17 = (f32[1,16,256]{2,1,0:T(8,128)S(1)}, f32[1,16,256]{2,1,0:T(8,128)}, u32[]{:S(2)}) copy-start(f32[1,16,256]{2,1,0:T(8,128)} %get-tuple-element.106) | copy-start | bytes 49156
  336.6 8.3 %copy-start.18 = (f32[1,16,256]{2,1,0:T(8,128)S(1)}, f32[1,16,256]{2,1,0:T(8,128)}, u32[]{:S(2)}) copy-start(f32[1,16,256]{2,1,0:T(8,128)} %get-tuple-element.101) | copy-start | bytes 49156
  336.6 8.3 %copy-start.19 = (f32[1,16,256]{2,1,0:T(8,128)S(1)}, f32[1,16,256]{2,1,0:T(8,128)}, u32[]{:S(2)}) copy-start(f32[1,16,256]{2,1,0:T(8,128)} %get-tuple-element.108) | copy-start | bytes 49156
  341.2 14.6 %all-to-all-start.4 = ((f32[4,1,43008]{2,1,0:T(1,128)}), f32[4,1,43008]{2,1,0:T(1,128)S(1)}, u32[]{:S(2)}, u32[]{:S(2)}) async-start(f32[4,1,43008]{2,1,0:T(1,128)} %reshape.200), calls=%async_computation.4 | async-start | bytes 1376256 | tf_op jit(solution)/shard_map/all_to_all | solution.py:62
  (8 other events, 13.0 us)
Sparse Core Ops, SparseCore 0:
  9.8 22.0 all-gather.1
where the time goes:
time: 375 us; the launch traced here: 368 us
  waiting for transfers between devices  128 us (34%)
  local copies, waits for them, and re-layouts  97.7 us (26%)
  other arithmetic  51.9 us (14%)
  starting transfers between devices  42.2 us (11%)
  matrix products  33.8 us (9%)
  between operations  15.1 us (4%)
    ppermute x2, waiting for transfers between devices, extended_2(): lax.ppermute(tail, axis, [(i, (i + 1) % count) for i in range(count)])  67.7 us
    concatenate x1, local copies, waits for them, and re-layouts, extended_2(): jnp.concatenate([lax.ppermute(tail, axis, [(i, (i + 1) % count) for i in...  26.7 us
    all_gather x1, waiting for transfers between devices, on_device(): gathered = lax.all_gather(features, 'chan', axis=0, tiled=True)  24 us
    unnamed x61, local copies, waits for them, and re-layouts  19.6 us
    all_to_all x2, starting transfers between devices, summed_on_arrival(): lax.all_to_all(tiles, axis, split_axis=0, concat_axis=0, tiled=True)  16.1 us
    ppermute x2, starting transfers between devices, extended_2(): lax.ppermute(head, axis, [((i + 1) % count, i) for i in range(count)])  14.2 us
    all_to_all x2, waiting for transfers between devices, from_everyone(): lax.all_to_all(jnp.broadcast_to(x[None], (count, *x.shape)), axis, 0, 0,...  12.4 us
    ppermute x2, waiting for transfers between devices, extended_2(): lax.ppermute(head, axis, [((i + 1) % count, i) for i in range(count)])  11.6 us
  transfers between devices with their start and end apart: 10, of which 9 were waited for; matrix products, arithmetic and copies ran while one was open for 15% of the time, Pallas kernels for 0%

commit v1 on v0

v1 whole, which is shorter than its diff:
```python
import functools
import math

import jax
import jax.numpy as jnp
from jax import lax
from jax.experimental import pallas as pl
from jax.experimental.pallas import tpu as pltpu
from jax.sharding import PartitionSpec as P

LMAX = 6
HALO = 128
M = 49
STEP = 7
ROUNDS = M // STEP
CAP = 10.0
MESH = pl.DeviceIdType.MESH
f32 = jnp.float32
bf16 = jnp.bfloat16
ANY = pl.BlockSpec(memory_space=pl.ANY)
VMEM = pl.BlockSpec(memory_space=pltpu.VMEM)
DMA = pltpu.SemaphoreType.DMA


def nn(a, b):
    return lax.dot_general(a, b, (((1,), (0,)), ((), ())), preferred_element_type=f32)


def nt(a, b):
    return lax.dot_general(a, b, (((1,), (1,)), ((), ())), preferred_element_type=f32)


def tn(a, b):
    return lax.dot_general(a, b, (((0,), (0,)), ((), ())), preferred_element_type=f32)


def degree_of(m):
    degree = jnp.int32(0)
    for low in range(1, LMAX + 1):
        degree = degree + (m >= low * low).astype(jnp.int32)
    return degree


def places():
    me = lax.axis_index("atom")
    chan = lax.axis_index("chan")
    count = lax.axis_size("atom")
    return me, chan, lax.rem(me + 1, count), lax.rem(me + count - 1, count), 1 - chan


def signal(sem, atom, chan):
    pl.semaphore_signal(sem, inc=1, device_id=(atom, chan), device_id_type=MESH)


def remote(src, dst, send, recv, atom, chan):
    return pltpu.make_async_remote_copy(
        src_ref=src, dst_ref=dst, send_sem=send, recv_sem=recv,
        device_id=(atom, chan), device_id_type=MESH)


def scores_kernel(feat, cot, w, q_out, k_out, fx_out, cx_out, s_out,
                  fx, cx, q, k, v, s,
                  loc_sem, out_sem, ps, pr, hs, hr, fs, fr, cs, cr):
    me, chan, right, left, other = places()
    cl = feat.shape[1]
    rows = pl.ds(pl.multiple_of(chan * cl, cl), cl)
    halves = (slice(0, HALO), slice(HALO, 2 * HALO))

    barrier = pltpu.get_barrier_semaphore()
    signal(barrier, left, chan)
    signal(barrier, right, chan)
    signal(barrier, me, other)
    own = pltpu.make_async_copy(feat, fx.at[0, :, rows, :], loc_sem.at[0])
    own.start()
    own_cot = pltpu.make_async_copy(cot, cx.at[0], loc_sem.at[1])
    own_cot.start()
    pl.semaphore_wait(barrier, 3)

    def part(i):
        return pl.ds(STEP * i, STEP)

    halo, fwd, mate = [], [], []
    for i in range(ROUNDS):
        for d, (to, src) in enumerate(((right, halves[1]), (left, halves[0]))):
            copy = remote(feat.at[part(i), :, src], fx.at[1, part(i), rows, halves[d]],
                          hs.at[d, i], hr.at[d, i], to, chan)
            copy.start()
            halo.append(copy)
            here = fx.at[1, part(i), rows, halves[d]]
            fwd.append(remote(here, here, fs.at[d, i], fr.at[d, i], me, other))
        copy = remote(feat.at[part(i)], fx.at[0, part(i), rows, :], ps.at[i], pr.at[i], me, other)
        copy.start()
        mate.append(copy)
    border = []
    for d, (to, src) in enumerate(((right, halves[1]), (left, halves[0]))):
        copy = remote(cot.at[:, :, src], cx.at[1, :, :, halves[d]], cs.at[d], cr.at[d], to, chan)
        copy.start()
        border.append(copy)

    def project(side, i):
        for u in range(STEP):
            m = STEP * i + u
            degree = math.isqrt(m)
            weight = w[:, degree].reshape(3 * cl, 2 * cl)
            out = nn(weight, fx[side, m]).astype(bf16)
            q[side, m] = out[:cl]
            k[side, m] = out[cl:2 * cl]
            v[side, m] = out[2 * cl:]

    def head(ref, side, h):
        return ref[side, :, 16 * h:16 * h + 16, :].reshape(16 * M, 2 * HALO)

    own.wait()
    for i in range(ROUNDS):
        mate[i].wait_recv()
        project(0, i)
    own_cot.wait()
    for h in range(4):
        s[h, :, 0:2 * HALO] = tn(head(q, 0, h), head(k, 0, h))
        s[4 + h, :, 0:2 * HALO] = tn(head(cx, 0, h), head(v, 0, h))
    outs = [pltpu.make_async_copy(fx.at[0], fx_out, out_sem.at[0])]
    outs[0].start()
    for i in range(ROUNDS):
        for d in range(2):
            halo[2 * i + d].wait_recv()
            fwd[2 * i + d].start()
        if i:
            for d in range(2):
                fwd[2 * i - 2 + d].wait_recv()
            project(1, i - 1)
    for d in range(2):
        fwd[2 * ROUNDS - 2 + d].wait_recv()
    project(1, ROUNDS - 1)
    outs.append(pltpu.make_async_copy(q, q_out, out_sem.at[1]))
    outs[1].start()
    outs.append(pltpu.make_async_copy(k, k_out, out_sem.at[2]))
    outs[2].start()
    for h in range(4):
        for row, left_ref, right_ref in ((h, q, k), (4 + h, cx, v)):
            a, b = head(left_ref, 0, h), head(right_ref, 1, h)
            for side in halves:
                s[row, side, 2 * HALO:] = tn(a[:, side], b[:, side])
    outs.append(pltpu.make_async_copy(s, s_out, out_sem.at[3]))
    outs[3].start()
    for copy in border:
        copy.wait_recv()
    outs.append(pltpu.make_async_copy(cx, cx_out, out_sem.at[4]))
    outs[4].start()
    for copy in halo + fwd + mate + border:
        copy.wait_send()
    for copy in outs:
        copy.wait()


def slots_kernel(s, bias, near, valid, grad_bias, band):
    heads, slots, atoms = bias.shape
    total = atoms * lax.axis_size("atom")
    scale = 1.0 / math.sqrt(16 * M)
    first = lax.axis_index("atom") * atoms
    t = near[...] - first + HALO
    t = jnp.where(t < 0, t + total, t)
    t = jnp.where(t >= total, t - total, t)
    j = t - HALO
    pos = jnp.where(j < 0, j + atoms + HALO, j)
    pos_t = jnp.concatenate([pos] * (2 * heads), axis=0).T
    block = pos_t // HALO
    lane = pos_t - block * HALO
    which = lax.broadcasted_iota(jnp.int32, pos_t.shape, 1) // slots
    picked = jnp.zeros(pos_t.shape, f32)
    for row in range(2 * heads):
        got = [jnp.take_along_axis(s[row, :, HALO * b:HALO * (b + 1)], lane, axis=1,
                                   mode="promise_in_bounds") for b in range(3)]
        got = jnp.where(block == 0, got[0], jnp.where(block == 1, got[1], got[2]))
        picked = jnp.where(which == row, got, picked)
    picked = picked.T
    live = valid[...] > 0
    raws, attns = [], []
    for h in range(heads):
        raw = scale * picked[slots * h:slots * (h + 1)]
        grad_attn = picked[slots * (heads + h):slots * (heads + h + 1)]
        squashed = jnp.tanh(raw / CAP)
        e = jnp.where(live, jnp.exp(CAP * squashed + bias[h]), 0.0)
        attn = e / jnp.sum(e, axis=0, keepdims=True)
        grad = attn * (grad_attn - jnp.sum(attn * grad_attn, axis=0, keepdims=True))
        grad_bias[h] = grad
        raws.append(scale * grad * (1.0 - squashed * squashed))
        attns.append(attn)
    parts = raws + attns
    sums = [jnp.zeros_like(x) for x in parts]
    for t in range(slots):
        same = pos == pos[t:t + 1]
        sums = [a + jnp.where(same, x[t:t + 1], 0.0) for a, x in zip(sums, parts)]
    spread = jnp.concatenate(sums, axis=0).T
    for b in range(3):
        here = lax.broadcasted_iota(jnp.int32, (atoms, HALO), 1) + HALO * b
        slot = jnp.full((atoms, HALO), -1, jnp.int32)
        for t in range(slots):
            slot = jnp.where(pos_t[:, t:t + 1] == here, t, slot)
        there = slot >= 0
        slot = jnp.maximum(slot, 0)
        cols = slice(HALO * b, HALO * (b + 1))
        for row in range(2 * heads):
            x = jnp.take_along_axis(spread, slot + slots * row, axis=1, mode="promise_in_bounds")
            x = jnp.where(there, x, 0.0)
            hi = x.astype(bf16)
            if row < heads:
                band[row, :, cols] = hi
                band[heads + row, :, cols] = (x - hi.astype(f32)).astype(bf16)
            else:
                band[heads + row, :, cols] = hi


def grads_kernel(band, q_in, k_in, cx_in, fx_in, w, gf, gw_out,
                 p, pr, q, k, cx, fx, g, wc, gw, part, arrived,
                 loc_sem, out_sem, bs, br, ms, mr):
    me, chan, right, left, other = places()
    cl = gf.shape[1]
    halves = (slice(0, HALO), slice(HALO, 2 * HALO))
    edge = slice(2 * HALO, 3 * HALO)
    loads = [pltpu.make_async_copy(src, dst, loc_sem.at[i]) for i, (src, dst) in enumerate(
        ((band, p), (k_in, k), (q_in, q), (cx_in, cx), (fx_in, fx)))]
    for copy in loads:
        copy.start()
    barrier = pltpu.get_barrier_semaphore()
    signal(barrier, left, chan)
    signal(barrier, right, chan)
    signal(barrier, me, other)
    pl.semaphore_wait(barrier, 3)
    border = []
    for d, (to, src) in enumerate(((right, halves[1]), (left, halves[0]))):
        copy = remote(band.at[:, src, edge], pr.at[d], bs.at[d], br.at[d], to, chan)
        copy.start()
        border.append(copy)
    for degree in range(LMAX + 1):
        wc[degree] = w[:, degree].reshape(3 * cl, 2 * cl).T
    gw[...] = jnp.zeros_like(gw)

    def head(ref, side, h):
        return ref[side, :, 16 * h:16 * h + 16, :].reshape(16 * M, 2 * HALO)

    def put(kind, h, value):
        first = kind * cl + 16 * h
        g[:, first:first + 16, :] = value.astype(bf16).reshape(M, 16, 2 * HALO)

    loads[0].wait()
    loads[1].wait()
    for h in range(4):
        own, rim = head(k, 0, h), head(k, 1, h)
        total = nt(own, p[h, :, 0:2 * HALO]) + nt(own, p[4 + h, :, 0:2 * HALO])
        sides = [nt(rim[:, side], p[h, side, edge]) + nt(rim[:, side], p[4 + h, side, edge])
                 for side in halves]
        put(0, h, total + jnp.concatenate(sides, axis=1))
    loads[2].wait()
    loads[3].wait()
    for copy in border:
        copy.wait_recv()
    for h in range(4):
        for kind, ref, terms in ((1, q, (h, 4 + h)), (2, cx, (8 + h,))):
            own, rim = head(ref, 0, h), head(ref, 1, h)
            total = sum(nn(own, p[t, :, 0:2 * HALO]) for t in terms)
            sides = [sum(nn(rim[:, side], pr[d, t]) for t in terms)
                     for d, side in enumerate(halves)]
            put(kind, h, total + jnp.concatenate(sides, axis=1))
    loads[4].wait()
    for degree in range(LMAX + 1):
        total = None
        for m in range(degree * degree, (degree + 1) * (degree + 1)):
            term = nt(g[m], fx[m])
            total = term if total is None else total + term
        for kind in range(3):
            first = (kind * (LMAX + 1) + degree) * cl
            gw[first:first + cl, :] = total[kind * cl:(kind + 1) * cl]
    out = pltpu.make_async_copy(gw, gw_out, out_sem.at[0])
    out.start()
    theirs = pl.ds(pl.multiple_of(other * cl, cl), cl)
    mine = pl.ds(pl.multiple_of(chan * cl, cl), cl)
    mate = []
    for i in range(ROUNDS):
        for u in range(STEP):
            m = STEP * i + u
            part[m] = nn(wc[math.isqrt(m)], g[m])
        rows = pl.ds(STEP * i, STEP)
        copy = remote(part.at[rows, theirs, :], arrived.at[rows], ms.at[i], mr.at[i], me, other)
        copy.start()
        mate.append(copy)
    for i in range(ROUNDS):
        mate[i].wait_recv()
        for u in range(STEP):
            m = STEP * i + u
            gf[m] = (part[m, mine, :] + arrived[m]).astype(bf16)
    for copy in border + mate:
        copy.wait_send()
    out.wait()


def total_kernel(plane, gw, out, near, red, far, last, fin,
                 loc_sem, as_, ar, zs, zr, gs, gr):
    me, chan = lax.axis_index("atom"), lax.axis_index("chan")
    deep = lax.axis_size("atom") // plane
    size = red.shape[0]
    z, xy = me // plane, lax.rem(me, plane)
    beside = [lax.rem(xy + d, plane) for d in range(plane)]
    behind = [lax.rem(z + d, deep) for d in range(deep)]

    def rows(i):
        return pl.ds(pl.multiple_of(i * size, 8), size)

    barrier = pltpu.get_barrier_semaphore()
    for d in range(1, plane):
        signal(barrier, z * plane + beside[d], chan)
    for d in range(1, deep):
        signal(barrier, behind[d] * plane + xy, chan)
    own = pltpu.make_async_copy(gw.at[rows(xy)], near.at[xy], loc_sem.at[0])
    own.start()
    pl.semaphore_wait(barrier, plane + deep - 2)
    first = []
    for d in range(1, plane):
        copy = remote(gw.at[rows(beside[d])], near.at[xy], as_.at[d], ar.at[d],
                      z * plane + beside[d], chan)
        copy.start()
        first.append(copy)
    own.wait()
    for copy in first:
        copy.wait_recv()
    total = near[0]
    for i in range(1, plane):
        total = total + near[i]
    red[...] = total
    second = []
    for d in range(1, deep):
        copy = remote(red, far.at[z], zs.at[d], zr.at[d], behind[d] * plane + xy, chan)
        copy.start()
        second.append(copy)
    far[z] = total
    for copy in second:
        copy.wait_recv()
    total = far[0]
    for i in range(1, deep):
        total = total + far[i]
    last[...] = total
    third = []
    for d in range(1, plane):
        copy = remote(last, fin.at[rows(xy)], gs.at[d], gr.at[d], z * plane + beside[d], chan)
        copy.start()
        third.append(copy)
    fin[rows(xy)] = total
    for copy in third:
        copy.wait_recv()
    for copy in first + second + third:
        copy.wait_send()
    out[...] = fin[0:out.shape[0]]


def params(collective=None, limit=60):
    more = {} if collective is None else {"collective_id": collective, "has_side_effects": True}
    return pltpu.CompilerParams(vmem_limit_bytes=limit * 1024 * 1024, **more)


def on_device(features, weights, cotangent, edge_bias, neighbours, valid_mask):
    cl, _, atoms = features.shape
    heads, slots, _ = edge_bias.shape
    feat = jnp.transpose(features, (1, 0, 2))
    cot = jnp.transpose(cotangent, (1, 0, 2))
    w = jnp.transpose(weights, (0, 1, 3, 2))
    S = jax.ShapeDtypeStruct
    both = (2, M, cl, atoms)
    wide = atoms + HALO
    q, k, fx, cx, s = pl.pallas_call(
        scores_kernel,
        out_shape=(S(both, bf16), S(both, bf16), S((M, 2 * cl, atoms), bf16), S(both, bf16),
                   S((2 * heads, atoms, wide), f32)),
        in_specs=[ANY, ANY, VMEM],
        out_specs=(ANY,) * 5,
        scratch_shapes=[
            pltpu.VMEM((2, M, 2 * cl, atoms), bf16), pltpu.VMEM(both, bf16),
            pltpu.VMEM(both, bf16), pltpu.VMEM(both, bf16), pltpu.VMEM(both, bf16),
            pltpu.VMEM((2 * heads, atoms, wide), f32),
            DMA((2,)), DMA((5,)), DMA((ROUNDS,)), DMA((ROUNDS,)),
            DMA((2, ROUNDS)), DMA((2, ROUNDS)), DMA((2, ROUNDS)), DMA((2, ROUNDS)),
            DMA((2,)), DMA((2,))],
        compiler_params=params(0), name="scores",
    )(feat, cot, w)
    grad_bias, band = pl.pallas_call(
        slots_kernel,
        out_shape=(S(edge_bias.shape, f32), S((3 * heads, atoms, wide), bf16)),
        in_specs=[VMEM] * 4,
        out_specs=(VMEM, VMEM),
        compiler_params=params(), name="slots",
    )(s, edge_bias, neighbours, valid_mask)
    kinds = 3 * (LMAX + 1) * cl
    plane = 16
    size = -(-kinds // (8 * plane)) * 8
    gf, gw = pl.pallas_call(
        grads_kernel,
        out_shape=(S((M, cl, atoms), bf16), S((plane * size, 2 * cl), f32)),
        in_specs=[ANY] * 5 + [VMEM],
        out_specs=(VMEM, ANY),
        scratch_shapes=[
            pltpu.VMEM((3 * heads, atoms, wide), bf16), pltpu.VMEM((2, 3 * heads, HALO, HALO), bf16),
            pltpu.VMEM(both, bf16), pltpu.VMEM(both, bf16), pltpu.VMEM(both, bf16),
            pltpu.VMEM((M, 2 * cl, atoms), bf16), pltpu.VMEM((M, 3 * cl, atoms), bf16),
            pltpu.VMEM((LMAX + 1, 2 * cl, 3 * cl), bf16), pltpu.VMEM((plane * size, 2 * cl), f32),
            pltpu.VMEM((M, 2 * cl, atoms), f32), pltpu.VMEM((M, cl, atoms), f32),
            DMA((5,)), DMA((1,)), DMA((2,)), DMA((2,)), DMA((ROUNDS,)), DMA((ROUNDS,))],
        compiler_params=params(1), name="grads",
    )(band, q, k, cx, fx, w)
    deep = lax.axis_size("atom") // plane
    total = pl.pallas_call(
        functools.partial(total_kernel, plane),
        out_shape=S((kinds, 2 * cl), f32),
        in_specs=[ANY],
        out_specs=VMEM,
        scratch_shapes=[
            pltpu.VMEM((plane, size, 2 * cl), f32), pltpu.VMEM((size, 2 * cl), f32),
            pltpu.VMEM((deep, size, 2 * cl), f32), pltpu.VMEM((size, 2 * cl), f32),
            pltpu.VMEM((plane * size, 2 * cl), f32),
            DMA((1,)), DMA((plane,)), DMA((plane,)), DMA((deep,)), DMA((deep,)),
            DMA((plane,)), DMA((plane,))],
        compiler_params=params(2, 16), name="total",
    )(gw)
    grad_weights = jnp.transpose(total.reshape(3, LMAX + 1, cl, 2 * cl), (0, 1, 3, 2))
    return jnp.transpose(gf, (1, 0, 2)), grad_weights, grad_bias


def solution(mesh):
    return jax.shard_map(
        on_device,
        mesh=mesh,
        in_specs=(P("chan", None, "atom"), P(None, None, None, "chan"), P("chan", None, "atom"),
                  P("chan", None, "atom"), P(None, "atom"), P(None, "atom")),
        out_specs=(P("chan", None, "atom"), P(None, None, None, "chan"), P("chan", None, "atom")),
        check_vma=False,
    )
```

time: 375 us -> 129 us (0.34)
  the two profiles are of different devices: /device:TPU:1 before, /device:TPU:65 now
where the time goes in v1:
time: 129 us
  Pallas kernels  123 us (95%)
  local copies, waits for them, and re-layouts  4.7 us (4%)
    pallas_call x1, Pallas kernels, on_device(): pl.pallas_call(scores_kernel, out_shape=(S(both, bf16), S(both, bf16), S(...  43.8 us
    pallas_call x1, Pallas kernels, on_device(): pl.pallas_call(functools.partial(total_kernel, plane), out_shape=S((kinds...  41.1 us
    pallas_call x1, Pallas kernels, on_device(): pl.pallas_call(grads_kernel, out_shape=(S((M, cl, atoms), bf16), S((plane...  29.5 us
    pallas_call x1, Pallas kernels, on_device(): pl.pallas_call(slots_kernel, out_shape=(S(edge_bias.shape, f32), S((3 * h...  9.11 us
    unnamed x4, local copies, waits for them, and re-layouts  4.7 us

profile of v1, /device:TPU:65, one launch (start us, length us, event | category | flops | bytes accessed | tf_op | source)
XLA Modules:
  0.0 128.8 jit_solution(8147452977927037102)
XLA Ops:
  0.6 43.8 %scores.1 = (bf16[2,49,64,256]{3,2,1,0:T(8,128)(2,1)}, bf16[2,49,64,256]{3,2,1,0:T(8,128)(2,1)}, bf16[49,128,256]{2,1,0:T(8,128)(2,1)}, bf16[2,49,64,256]{3,2,1,0:T(8,128)(2,1)}, f32[8,256,384]{2,1,0:T(8,128)}) custom-call(bf16[49,64,256]{2,1,0:T(8,128)(2,1)} %bitcast.8, bf16[49,64,256]{2,1,0:T(8,128)(2,1)} %bitcast.9, bf16[3,7,64,128]{3,2,1,0:T(8,128)(2,1)} %bitcast.11), custom_call_target="tpu_custom_call" | custom-call | tf_op jit(solution)/shard_map/scores/pallas_call | solution.py:368
  44.4 9.1 %slots.1 = (f32[4,16,256]{2,1,0:T(8,128)}, bf16[12,256,384]{2,1,0:T(8,128)(2,1)}) custom-call(f32[8,256,384]{2,1,0:T(8,128)} %get-tuple-element.12.s, f32[4,16,256]{2,1,0:T(8,128)} %bias.1, s32[16,256]{1,0:T(8,128)} %near.1, s32[16,256]{1,0:T(8,128)} %valid.1), custom_call_target="tpu_custom_call" | custom-call | tf_op jit(solution)/shard_map/slots/pallas_call | solution.py:383
  53.5 29.5 %grads.1 = (bf16[49,64,256]{2,1,0:T(8,128)(2,1)}, f32[1408,128]{1,0:T(8,128)}) custom-call(bf16[12,256,384]{2,1,0:T(8,128)(2,1)} %get-tuple-element.13.band, bf16[2,49,64,256]{3,2,1,0:T(8,128)(2,1)} %get-tuple-element.14.q_in, bf16[2,49,64,256]{3,2,1,0:T(8,128)(2,1)} %get-tuple-element.15.k_in, bf16[2,49,64,256]{3,2,1,0:T(8,128)(2,1)} %get-tuple-element.16.cx_in, ...), custom_call_target="tpu_custom_call" | custom-call | tf_op jit(solution)/shard_map/grads/pallas_call | solution.py:393
  83.0 0.0 copy-start
  83.0 1.1 copy-done
  84.1 41.1 %total.1 = f32[1344,128]{1,0:T(8,128)S(1)} custom-call(f32[1408,128]{1,0:T(8,128)S(1)} %copy-done), custom_call_target="tpu_custom_call" | custom-call | tf_op jit(solution)/shard_map/total/pallas_call | solution.py:408
  125.2 2.8 %copy.11 = bf16[64,49,256]{2,0,1:T(8,128)(2,1)} copy(bf16[64,49,256]{2,0,1:T(8,128)(2,1)} %bitcast.10) | data formatting | bytes 3211264
  128.0 0.8 copy.12
Async XLA Ops:
  83.0 1.1 copy-start

commit v2 on v1

v2 whole, which is shorter than its diff:
```python
import functools
import math

import jax
import jax.numpy as jnp
from jax import lax
from jax.experimental import pallas as pl
from jax.experimental.pallas import tpu as pltpu
from jax.sharding import PartitionSpec as P

LMAX = 6
HALO = 128
M = 49
STEP = 7
ROUNDS = M // STEP
CAP = 10.0
MESH = pl.DeviceIdType.MESH
f32 = jnp.float32
bf16 = jnp.bfloat16
ANY = pl.BlockSpec(memory_space=pl.ANY)
VMEM = pl.BlockSpec(memory_space=pltpu.VMEM)
DMA = pltpu.SemaphoreType.DMA


def nn(a, b):
    return lax.dot_general(a, b, (((1,), (0,)), ((), ())), preferred_element_type=f32)


def nt(a, b):
    return lax.dot_general(a, b, (((1,), (1,)), ((), ())), preferred_element_type=f32)


def tn(a, b):
    return lax.dot_general(a, b, (((0,), (0,)), ((), ())), preferred_element_type=f32)


def places():
    me = lax.axis_index("atom")
    chan = lax.axis_index("chan")
    count = lax.axis_size("atom")
    return me, chan, lax.rem(me + 1, count), lax.rem(me + count - 1, count), 1 - chan


def signal(sem, atom, chan):
    pl.semaphore_signal(sem, inc=1, device_id=(atom, chan), device_id_type=MESH)


def remote(src, dst, send, recv, atom, chan):
    return pltpu.make_async_remote_copy(
        src_ref=src, dst_ref=dst, send_sem=send, recv_sem=recv,
        device_id=(atom, chan), device_id_type=MESH)


def layer_kernel(plane, feat, cot, w, bias, near, valid, gf_out, gw_out, grad_bias,
                 fx, cx, q, k, v, s, nx, spread, xs, p, pr, g, part, arrived, gf, wc, gw,
                 a_near, a_red, a_far, a_last, b_near, b_red, b_far, b_last, fin,
                 loc_sem, out_sem, ns, nr, ps, pr_sem, hs, hr, fs, fr, cs, cr, xss, xsr, ms, mr,
                 a1s, a1r, a2s, a2r, a3s, a3r, b1s, b1r, b2s, b2r, b3s, b3r):
    me, chan, right, left, other = places()
    heads, slots, atoms = bias.shape
    cl = feat.shape[1]
    count = lax.axis_size("atom")
    deep = count // plane
    z, xy = me // plane, lax.rem(me, plane)
    beside = [z * plane + lax.rem(xy + d, plane) for d in range(plane)]
    behind = [lax.rem(z + d, deep) * plane + xy for d in range(deep)]
    size = a_red.shape[0]
    rows = pl.ds(pl.multiple_of(chan * cl, cl), cl)
    theirs = pl.ds(pl.multiple_of(other * cl, cl), cl)
    halves = (slice(0, HALO), slice(HALO, 2 * HALO))
    edge = slice(2 * HALO, 3 * HALO)
    ways = ((right, halves[1]), (left, halves[0]))

    def piece(i, base=0):
        return pl.ds(pl.multiple_of(base + i * size, 8), size)

    def chunk(i):
        return pl.ds(STEP * i, STEP)

    def head(ref, side, h):
        return ref[side, :, 16 * h:16 * h + 16, :].reshape(16 * M, 2 * HALO)

    barrier = pltpu.get_barrier_semaphore()
    signal(barrier, left, chan)
    signal(barrier, right, chan)
    signal(barrier, me, other)
    for peer in beside[1:] + behind[1:]:
        signal(barrier, peer, chan)
    own = pltpu.make_async_copy(feat, fx.at[0, :, rows, :], loc_sem.at[0])
    own.start()
    own_cot = pltpu.make_async_copy(cot, cx.at[0], loc_sem.at[1])
    own_cot.start()
    for degree in range(LMAX + 1):
        wc[degree] = w[:, degree].reshape(3 * cl, 2 * cl).T
    pl.semaphore_wait(barrier, plane + deep + 1)

    sent = []

    def go(copy):
        copy.start()
        sent.append(copy)
        return copy

    table = [go(remote(near.at[:, src], nx.at[d], ns.at[d], nr.at[d], to, chan))
             for d, (to, src) in enumerate(ways)]
    halo, fwd, mate = [], [], []
    for i in range(ROUNDS):
        for d, (to, src) in enumerate(ways):
            here = fx.at[1, chunk(i), rows, halves[d]]
            halo.append(go(remote(feat.at[chunk(i), :, src], here, hs.at[d, i], hr.at[d, i],
                                  to, chan)))
            fwd.append(remote(here, here, fs.at[d, i], fr.at[d, i], me, other))
        mate.append(go(remote(feat.at[chunk(i)], fx.at[0, chunk(i), rows, :],
                              ps.at[i], pr_sem.at[i], me, other)))
    cuts = (slice(0, 28), slice(28, M))

    def send_cot(n):
        return [go(remote(cot.at[cuts[n], :, src], cx.at[1, cuts[n], :, halves[d]],
                          cs.at[d, n], cr.at[d, n], to, chan))
                for d, (to, src) in enumerate(ways)]

    border = send_cot(0)

    def project(side, i):
        for u in range(STEP):
            m = STEP * i + u
            weight = w[:, math.isqrt(m)].reshape(3 * cl, 2 * cl)
            out = nn(weight, fx[side, m]).astype(bf16)
            q[side, m] = out[:cl]
            k[side, m] = out[cl:2 * cl]
            v[side, m] = out[2 * cl:]

    own.wait()
    for i in range(ROUNDS):
        mate[i].wait_recv()
        project(0, i)
    own_cot.wait()
    for h in range(heads):
        s[h, :, 0:atoms] = tn(head(q, 0, h), head(k, 0, h))
        s[heads + h, :, 0:atoms] = tn(head(cx, 0, h), head(v, 0, h))

    total = atoms * count
    first = me * atoms

    def local(x):
        t = x - first + HALO
        t = jnp.where(t < 0, t + total, t)
        return jnp.where(t >= total, t - total, t) - HALO

    def turned(x):
        return jnp.concatenate([x] * (2 * heads), axis=0).T

    def slot_of(pos_t, low):
        here = lax.broadcasted_iota(jnp.int32, (pos_t.shape[0], HALO), 1) + low
        slot = jnp.full(here.shape, -1, jnp.int32)
        for t in range(slots):
            slot = jnp.where(pos_t[:, t:t + 1] == here, t, slot)
        return slot

    def spread_out(values, slot, write):
        there = slot >= 0
        slot = jnp.maximum(slot, 0)
        for row in range(2 * heads):
            x = jnp.take_along_axis(values, slot + slots * row, axis=1,
                                    mode="promise_in_bounds")
            x = jnp.where(there, x, 0.0)
            hi = x.astype(bf16)
            write(row, hi)
            write(2 * heads + row, (x - hi.astype(f32)).astype(bf16))

    j = local(near[...])
    pos = jnp.where(j < 0, j + atoms + HALO, j)
    pos_t = turned(pos)

    for i in range(ROUNDS):
        for d in range(2):
            halo[2 * i + d].wait_recv()
            go(fwd[2 * i + d])
        if i:
            for d in range(2):
                fwd[2 * i - 2 + d].wait_recv()
            project(1, i - 1)
    for d in range(2):
        fwd[2 * ROUNDS - 2 + d].wait_recv()
    project(1, ROUNDS - 1)
    for h in range(heads):
        for row, left_ref, right_ref in ((h, q, k), (heads + h, cx, v)):
            a, b = head(left_ref, 0, h), head(right_ref, 1, h)
            for side in halves:
                s[row, side, edge] = tn(a[:, side], b[:, side])

    scale = 1.0 / math.sqrt(16 * M)
    block = pos_t // HALO
    lane = pos_t - block * HALO
    which = lax.broadcasted_iota(jnp.int32, pos_t.shape, 1) // slots
    picked = jnp.zeros(pos_t.shape, f32)
    for row in range(2 * heads):
        got = [jnp.take_along_axis(s[row, :, HALO * b:HALO * (b + 1)], lane, axis=1,
                                   mode="promise_in_bounds") for b in range(3)]
        got = jnp.where(block == 0, got[0], jnp.where(block == 1, got[1], got[2]))
        picked = jnp.where(which == row, got, picked)
    picked = picked.T
    live = valid[...] > 0
    raws, attns = [], []
    for h in range(heads):
        raw = scale * picked[slots * h:slots * (h + 1)]
        grad_attn = picked[slots * (heads + h):slots * (heads + h + 1)]
        squashed = jnp.tanh(raw / CAP)
        e = jnp.where(live, jnp.exp(CAP * squashed + bias[h]), 0.0)
        attn = e / jnp.sum(e, axis=0, keepdims=True)
        grad = attn * (grad_attn - jnp.sum(attn * grad_attn, axis=0, keepdims=True))
        grad_bias[h] = grad
        raws.append(scale * grad * (1.0 - squashed * squashed))
        attns.append(attn)
    parts = raws + attns
    sums = [jnp.zeros_like(x) for x in parts]
    for t in range(slots):
        same = pos == pos[t:t + 1]
        sums = [a + jnp.where(same, x[t:t + 1], 0.0) for a, x in zip(sums, parts)]
    spread[...] = jnp.concatenate(sums, axis=0).T
    rims = [go(remote(spread.at[src], xs.at[d], xss.at[d], xsr.at[d], to, chan))
            for d, (to, src) in enumerate(ways)]
    border += send_cot(1)

    for b in range(3):
        def write(row, x, b=b):
            p[row, :, HALO * b:HALO * (b + 1)] = x
        spread_out(spread[...], slot_of(pos_t, HALO * b), write)

    def put(kind, h, value):
        low = kind * cl + 16 * h
        g[:, low:low + 16, :] = value.astype(bf16).reshape(M, 16, atoms)

    def keep(kind, h):
        low = (kind - 1) * cl + 16 * h
        return slice(low, low + 16)

    for h in range(heads):
        mine, rim = head(k, 0, h), head(k, 1, h)
        terms = (h, 2 * heads + h)
        inner = sum(nt(mine, p[t, :, 0:atoms]) for t in terms)
        sides = [sum(nt(rim[:, side], p[t, side, edge]) for t in terms) for side in halves]
        put(0, h, inner + jnp.concatenate(sides, axis=1))
    for degree in range(LMAX + 1):
        acc = None
        for m in range(degree * degree, (degree + 1) * (degree + 1)):
            term = nt(g[m, 0:cl], fx[0, m])
            acc = term if acc is None else acc + term
        gw[degree * cl:(degree + 1) * cl, :] = acc
    b_one = []
    for d in range(1, deep):
        to = lax.rem(z + d, deep)
        b_one.append(go(remote(gw.at[piece(to)], b_near.at[z], b1s.at[d], b1r.at[d],
                               behind[d], chan)))
    b_near[z] = gw[piece(z)]
    for h in range(heads):
        for kind, ref in ((1, q), (2, cx)):
            mine = head(ref, 0, h)
            base = (kind - 1) * heads + h
            inner = sum(nn(mine, p[t, :, 0:atoms]) for t in (base, 2 * heads + base))
            part[:, keep(kind, h), :] = inner.reshape(M, 16, atoms)
    for d in range(2):
        table[d].wait_recv()
        rims[d].wait_recv()

        def write(row, x, d=d):
            pr[d, row] = x
        spread_out(xs[d], slot_of(turned(local(nx[d])), HALO * d), write)

    def finish(kind, ref):
        for h in range(heads):
            rim = head(ref, 1, h)
            base = (kind - 1) * heads + h
            sides = [sum(nn(rim[:, side], pr[d, t]) for t in (base, 2 * heads + base))
                     for d, side in enumerate(halves)]
            inner = part[:, keep(kind, h), :].reshape(16 * M, atoms)
            put(kind, h, inner + jnp.concatenate(sides, axis=1))

    finish(1, q)
    for copy in border:
        copy.wait_recv()
    finish(2, cx)
    for copy in b_one:
        copy.wait_recv()
    b_red[...] = sum(b_near[i] for i in range(deep))
    b_two = [go(remote(b_red, b_far.at[xy], b2s.at[d], b2r.at[d], beside[d], chan))
             for d in range(1, plane)]
    b_far[xy] = b_red[...]
    kinds = LMAX + 1
    for degree in range(kinds):
        acc = None
        for m in range(degree * degree, (degree + 1) * (degree + 1)):
            term = nt(g[m, cl:3 * cl], fx[0, m])
            acc = term if acc is None else acc + term
        for kind in (1, 2):
            low = (kind * kinds + degree) * cl
            gw[low:low + cl, :] = acc[(kind - 1) * cl:kind * cl]
    base = kinds * cl
    a_one = []
    for d in range(1, plane):
        to = lax.rem(xy + d, plane)
        a_one.append(go(remote(gw.at[piece(to, base)], a_near.at[xy], a1s.at[d], a1r.at[d],
                               beside[d], chan)))
    a_near[xy] = gw[piece(xy, base)]

    def feature_terms(i):
        for u in range(STEP):
            m = STEP * i + u
            part[m] = nn(wc[math.isqrt(m)], g[m])
        return go(remote(part.at[chunk(i), theirs, :], arrived.at[chunk(i)],
                         ms.at[i], mr.at[i], me, other))

    swap = [feature_terms(i) for i in range(ROUNDS)]
    for copy in a_one:
        copy.wait_recv()
    a_red[...] = sum(a_near[i] for i in range(plane))
    a_two = [go(remote(a_red, a_far.at[z], a2s.at[d], a2r.at[d], behind[d], chan))
             for d in range(1, deep)]
    a_far[z] = a_red[...]
    for copy in b_two:
        copy.wait_recv()
    b_last[...] = sum(b_far[i] for i in range(plane))
    b_three = [go(remote(b_last, fin.at[piece(z)], b3s.at[d], b3r.at[d], behind[d], chan))
               for d in range(1, deep)]
    fin[piece(z)] = b_last[...]
    for i in range(2):
        swap[i].wait_recv()
    for copy in a_two:
        copy.wait_recv()
    a_last[...] = sum(a_far[i] for i in range(deep))
    a_three = [go(remote(a_last, fin.at[piece(xy, base)], a3s.at[d], a3r.at[d], beside[d], chan))
               for d in range(1, plane)]
    fin[piece(xy, base)] = a_last[...]
    outs = []
    for i in range(ROUNDS):
        if i > 1:
            swap[i].wait_recv()
        for u in range(STEP):
            m = STEP * i + u
            gf[m] = (part[m, rows, :] + arrived[m]).astype(bf16)
        outs.append(pltpu.make_async_copy(gf.at[chunk(i)], gf_out.at[chunk(i)], out_sem.at[i]))
        outs[i].start()
    for copy in b_three + a_three:
        copy.wait_recv()
    gw_out[...] = fin[...]
    for copy in sent:
        copy.wait_send()
    for copy in outs:
        copy.wait()


def on_device(features, weights, cotangent, edge_bias, neighbours, valid_mask):
    cl, _, atoms = features.shape
    heads, slots, _ = edge_bias.shape
    feat = jnp.transpose(features, (1, 0, 2))
    cot = jnp.transpose(cotangent, (1, 0, 2))
    w = jnp.transpose(weights, (0, 1, 3, 2))
    S = jax.ShapeDtypeStruct
    both = (2, M, cl, atoms)
    wide = atoms + HALO
    kinds = 3 * (LMAX + 1) * cl
    plane = 16
    deep = lax.axis_size("atom") // plane
    size = (LMAX + 1) * cl // deep
    V = pltpu.VMEM
    row = (size, 2 * cl)
    gf, total, grad_bias = pl.pallas_call(
        functools.partial(layer_kernel, plane),
        out_shape=(S((M, cl, atoms), bf16), S((kinds, 2 * cl), f32), S(edge_bias.shape, f32)),
        in_specs=[ANY, ANY, VMEM, VMEM, VMEM, VMEM],
        out_specs=(ANY, VMEM, VMEM),
        scratch_shapes=[
            V((2, M, 2 * cl, atoms), bf16), V(both, bf16), V(both, bf16), V(both, bf16),
            V(both, bf16), V((2 * heads, atoms, wide), f32), V((2, slots, HALO), jnp.int32),
            V((atoms, HALO), f32), V((2, HALO, HALO), f32),
            V((4 * heads, atoms, wide), bf16), V((2, 4 * heads, HALO, HALO), bf16),
            V((M, 3 * cl, atoms), bf16), V((M, 2 * cl, atoms), f32), V((M, cl, atoms), f32),
            V((M, cl, atoms), bf16), V((LMAX + 1, 2 * cl, 3 * cl), bf16), V((kinds, 2 * cl), f32),
            V((plane, *row), f32), V(row, f32), V((deep, *row), f32), V(row, f32),
            V((deep, *row), f32), V(row, f32), V((plane, *row), f32), V(row, f32),
            V((kinds, 2 * cl), f32),
            DMA((2,)), DMA((ROUNDS,)), DMA((2,)), DMA((2,)), DMA((ROUNDS,)), DMA((ROUNDS,)),
            DMA((2, ROUNDS)), DMA((2, ROUNDS)), DMA((2, ROUNDS)), DMA((2, ROUNDS)),
            DMA((2, 2)), DMA((2, 2)), DMA((2,)), DMA((2,)), DMA((ROUNDS,)), DMA((ROUNDS,)),
            DMA((plane,)), DMA((plane,)), DMA((deep,)), DMA((deep,)), DMA((plane,)), DMA((plane,)),
            DMA((deep,)), DMA((deep,)), DMA((plane,)), DMA((plane,)), DMA((deep,)), DMA((deep,))],
        compiler_params=pltpu.CompilerParams(
            vmem_limit_bytes=62 * 1024 * 1024, collective_id=0, has_side_effects=True),
        name="layer",
    )(feat, cot, w, edge_bias, neighbours, valid_mask)
    grad_weights = jnp.transpose(total.reshape(3, LMAX + 1, cl, 2 * cl), (0, 1, 3, 2))
    return jnp.transpose(gf, (1, 0, 2)), grad_weights, grad_bias


def solution(mesh):
    return jax.shard_map(
        on_device,
        mesh=mesh,
        in_specs=(P("chan", None, "atom"), P(None, None, None, "chan"), P("chan", None, "atom"),
                  P("chan", None, "atom"), P(None, "atom"), P(None, "atom")),
        out_specs=(P("chan", None, "atom"), P(None, None, None, "chan"), P("chan", None, "atom")),
        check_vma=False,
    )
```

time: 129 us -> 90.4 us (0.70)
  the two profiles are of different devices: /device:TPU:65 before, /device:TPU:8 now
where the time goes in v2:
time: 90.4 us; the launch traced here: 90.2 us
  Pallas kernels  85.3 us (94%)
  local copies, waits for them, and re-layouts  4.31 us (5%)
    pallas_call x1, Pallas kernels, on_device(): pl.pallas_call(functools.partial(layer_kernel, plane), out_shape=(S((M, c...  85.3 us
    unnamed x7, local copies, waits for them, and re-layouts  4.31 us

profile of v2, /device:TPU:8, one launch (start us, length us, event | category | flops | bytes accessed | tf_op | source)
XLA Modules:
  0.0 90.2 jit_solution(16985205921162277658)
XLA Ops:
  0.6 85.3 %layer.1 = (bf16[49,64,256]{2,1,0:T(8,128)(2,1)}, f32[1344,128]{1,0:T(8,128)}, f32[4,16,256]{2,1,0:T(8,128)}) custom-call(bf16[49,64,256]{2,1,0:T(8,128)(2,1)} %bitcast.7, bf16[49,64,256]{2,1,0:T(8,128)(2,1)} %bitcast.8, bf16[3,7,64,128]{3,2,1,0:T(8,128)(2,1)} %bitcast.11, f32[4,16,256]{2,1,0:T(8,128)} %bias.1, s32[16,256]{1,0:T(8,128)} %near.1, s32[16,256]{1,0:T(8,128)} %valid.1), custom_call_target="tpu_custom_call" | custom-call | tf_op jit(solution)/shard_map/layer/pallas_call | solution.py:367
  85.9 0.0 copy-start
  85.9 0.0 copy-start.1
  85.9 2.8 %copy.12 = bf16[64,49,256]{2,0,1:T(8,128)(2,1)} copy(bf16[64,49,256]{2,0,1:T(8,128)(2,1)} %bitcast.9) | data formatting | bytes 3211264
  88.7 0.0 copy-done
  88.7 0.8 copy.13
  89.6 0.0 copy-done.1
  89.6 0.6 copy.14
Async XLA Ops:
  85.9 2.8 %copy-start = (f32[1344,128]{1,0:T(8,128)S(1)}, f32[1344,128]{1,0:T(8,128)}, u32[]{:S(2)}) copy-start(f32[1344,128]{1,0:T(8,128)} %get-tuple-element.7) | copy-start | bytes 2064388
  85.9 3.7 %copy-start.1 = (f32[4,16,256]{2,1,0:T(8,128)S(1)}, f32[4,16,256]{2,1,0:T(8,128)}, u32[]{:S(2)}) copy-start(f32[4,16,256]{2,1,0:T(8,128)} %get-tuple-element.14) | copy-start | bytes 196612

commit v3 on v2

v3 whole, which is shorter than its diff:
```python
import functools
import math

import jax
import jax.numpy as jnp
from jax import lax
from jax.experimental import pallas as pl
from jax.experimental.pallas import tpu as pltpu
from jax.sharding import PartitionSpec as P

LMAX = 6
HALO = 128
M = 49
STEP = 7
ROUNDS = M // STEP
CAP = 10.0
MESH = pl.DeviceIdType.MESH
f32 = jnp.float32
bf16 = jnp.bfloat16
ANY = pl.BlockSpec(memory_space=pl.ANY)
VMEM = pl.BlockSpec(memory_space=pltpu.VMEM)
DMA = pltpu.SemaphoreType.DMA


def nn(a, b):
    return lax.dot_general(a, b, (((1,), (0,)), ((), ())), preferred_element_type=f32)


def nt(a, b):
    return lax.dot_general(a, b, (((1,), (1,)), ((), ())), preferred_element_type=f32)


def tn(a, b):
    return lax.dot_general(a, b, (((0,), (0,)), ((), ())), preferred_element_type=f32)


def places():
    me = lax.axis_index("atom")
    chan = lax.axis_index("chan")
    count = lax.axis_size("atom")
    return me, chan, lax.rem(me + 1, count), lax.rem(me + count - 1, count), 1 - chan


def signal(sem, atom, chan):
    pl.semaphore_signal(sem, inc=1, device_id=(atom, chan), device_id_type=MESH)


def remote(src, dst, send, recv, atom, chan):
    return pltpu.make_async_remote_copy(
        src_ref=src, dst_ref=dst, send_sem=send, recv_sem=recv,
        device_id=(atom, chan), device_id_type=MESH)


def layer_kernel(plane, feat, cot, w, bias, near, valid, gf_out, gw_out, grad_bias,
                 fx, cx, q, k, v, s, nx, spread, xs, slot_own, slot_rim, p, pr, g, part, arrived,
                 gf, wc, gw, a_near, a_red, a_far, a_last, b_near, b_red, b_far, b_last, fin,
                 loc_sem, out_sem, ns, nr, ps, pr_sem, hs, hr, fs, fr, cs, cr, xss, xsr, ms, mr,
                 a1s, a1r, a2s, a2r, a3s, a3r, b1s, b1r, b2s, b2r, b3s, b3r):
    me, chan, right, left, other = places()
    heads, slots, atoms = bias.shape
    cl = feat.shape[1]
    count = lax.axis_size("atom")
    deep = count // plane
    z, xy = me // plane, lax.rem(me, plane)
    beside = [z * plane + lax.rem(xy + d, plane) for d in range(plane)]
    behind = [lax.rem(z + d, deep) * plane + xy for d in range(deep)]
    rows = pl.ds(pl.multiple_of(chan * cl, cl), cl)
    theirs = pl.ds(pl.multiple_of(other * cl, cl), cl)
    halves = (slice(0, HALO), slice(HALO, 2 * HALO))
    edge = slice(2 * HALO, 3 * HALO)
    ways = ((right, halves[1]), (left, halves[0]))

    def chunk(i):
        return pl.ds(STEP * i, STEP)

    def head(ref, side, h):
        return ref[side, :, 16 * h:16 * h + 16, :].reshape(16 * M, 2 * HALO)

    barrier = pltpu.get_barrier_semaphore()
    signal(barrier, left, chan)
    signal(barrier, right, chan)
    signal(barrier, me, other)
    for peer in beside[1:] + behind[1:]:
        signal(barrier, peer, chan)
    own = pltpu.make_async_copy(feat, fx.at[0, :, rows, :], loc_sem.at[0])
    own.start()
    own_cot = pltpu.make_async_copy(cot, cx.at[0], loc_sem.at[1])
    own_cot.start()
    pl.semaphore_wait(barrier, plane + deep + 1)

    sent = []

    def go(copy):
        copy.start()
        sent.append(copy)
        return copy

    table = [go(remote(near.at[:, src], nx.at[d], ns.at[d], nr.at[d], to, chan))
             for d, (to, src) in enumerate(ways)]
    halo, fwd, mate, late = [], [], [], []
    for i in range(ROUNDS):
        for d, (to, src) in enumerate(ways):
            here = fx.at[1, chunk(i), rows, halves[d]]
            halo.append(remote(feat.at[chunk(i), :, src], here, hs.at[d, i], hr.at[d, i],
                               to, chan))
            fwd.append(remote(here, here, fs.at[d, i], fr.at[d, i], me, other))
    for h in range(heads):
        at = slice(16 * h, 16 * h + 16)
        for d, (to, src) in enumerate(ways):
            late.append(remote(cot.at[:, at, src], cx.at[1, :, at, halves[d]],
                               cs.at[d, h], cr.at[d, h], to, chan))
    queue = halo + late

    def feed(n):
        if n > 1:
            for copy in queue[2 * n - 4:2 * n - 2]:
                copy.wait_send()
        for copy in queue[2 * n:2 * n + 2]:
            copy.start()

    def relay(i):
        for copy in halo[2 * i:2 * i + 2]:
            copy.wait_recv()
        for copy in fwd[2 * i:2 * i + 2]:
            go(copy)

    feed(0)
    feed(1)
    for i in range(ROUNDS):
        mate.append(go(remote(feat.at[chunk(i)], fx.at[0, chunk(i), rows, :],
                              ps.at[i], pr_sem.at[i], me, other)))

    def project(side, i):
        for u in range(STEP):
            m = STEP * i + u
            weight = w[:, math.isqrt(m)].reshape(3 * cl, 2 * cl)
            out = nn(weight, fx[side, m]).astype(bf16)
            q[side, m] = out[:cl]
            k[side, m] = out[cl:2 * cl]
            v[side, m] = out[2 * cl:]

    def own_scores(h):
        s[h, :, 0:atoms] = tn(head(q, 0, h), head(k, 0, h))
        s[heads + h, :, 0:atoms] = tn(head(cx, 0, h), head(v, 0, h))

    own.wait()
    for i in range(ROUNDS):
        mate[i].wait_recv()
        project(0, i)
        if i == 3:
            feed(2)
    feed(3)
    own_cot.wait()
    own_scores(0)
    own_scores(1)
    feed(4)
    own_scores(2)
    own_scores(3)
    for degree in range(LMAX + 1):
        wc[degree] = w[:, degree].reshape(3 * cl, 2 * cl).T
    feed(5)
    relay(0)
    relay(1)

    total = atoms * count
    first = me * atoms
    strip = 64

    def local(x):
        t = x - first + HALO
        t = jnp.where(t < 0, t + total, t)
        return jnp.where(t >= total, t - total, t) - HALO

    def turned(x):
        return jnp.concatenate([x] * (2 * heads), axis=0).T

    def slot_table(pos_t, low, ref):
        for r in range(0, pos_t.shape[0], strip):
            here = lax.broadcasted_iota(jnp.int32, (strip, HALO), 1) + low
            slot = jnp.full(here.shape, -1, jnp.int32)
            for t in range(slots):
                slot = jnp.where(pos_t[r:r + strip, t:t + 1] == here, t, slot)
            ref[r:r + strip, :] = slot

    def spread_out(values, table, write):
        for r in range(0, values.shape[0], strip):
            value = values[r:r + strip, :]
            slot = table[r:r + strip, :]
            there = slot >= 0
            slot = jnp.maximum(slot, 0)
            for row in range(2 * heads):
                x = jnp.take_along_axis(value, slot + slots * row, axis=1,
                                        mode="promise_in_bounds")
                x = jnp.where(there, x, 0.0)
                hi = x.astype(bf16)
                write(row, r, hi)
                write(2 * heads + row, r, (x - hi.astype(f32)).astype(bf16))

    j = local(near[...])
    pos = jnp.where(j < 0, j + atoms + HALO, j)
    pos_t = turned(pos)
    for b in range(3):
        slot_table(pos_t, HALO * b, slot_own.at[b])
    feed(6)
    relay(2)
    relay(3)
    for d in range(2):
        table[d].wait_recv()
        slot_table(turned(local(nx[d])), HALO * d, slot_rim.at[d])
    blank = jnp.zeros((4 * heads, HALO, HALO), bf16)
    p[:, 0:HALO, 3 * HALO:] = blank
    p[:, HALO:, 2 * HALO:3 * HALO] = blank
    pr[:, 0:HALO, HALO:] = blank
    pr[:, HALO:, 0:HALO] = blank
    gw[gw_out.shape[0]:, :] = jnp.zeros((gw.shape[0] - gw_out.shape[0], 2 * cl), f32)

    def rim_project(i):
        for copy in fwd[2 * i:2 * i + 2]:
            copy.wait_recv()
        project(1, i)

    feed(7)
    for i in range(3):
        rim_project(i)
    relay(4)
    rim_project(3)
    relay(5)
    rim_project(4)
    feed(8)
    relay(6)
    rim_project(5)
    rim_project(6)
    for h in range(heads):
        for row, left_ref, right_ref in ((h, q, k), (heads + h, cx, v)):
            a, b = head(left_ref, 0, h), head(right_ref, 1, h)
            for side in halves:
                s[row, side, edge] = tn(a[:, side], b[:, side])

    scale = 1.0 / math.sqrt(16 * M)
    strips = []
    for r in range(0, atoms, strip):
        at = pos_t[r:r + strip]
        block = at // HALO
        lane = at - block * HALO
        which = lax.broadcasted_iota(jnp.int32, at.shape, 1) // slots
        picked = jnp.zeros(at.shape, f32)
        for row in range(2 * heads):
            got = [jnp.take_along_axis(s[row, r:r + strip, HALO * b:HALO * (b + 1)], lane, axis=1,
                                       mode="promise_in_bounds") for b in range(3)]
            got = jnp.where(block == 0, got[0], jnp.where(block == 1, got[1], got[2]))
            picked = jnp.where(which == row, got, picked)
        strips.append(picked)
    picked = jnp.concatenate(strips, axis=0).T
    live = valid[...] > 0
    raws, attns = [], []
    for h in range(heads):
        raw = scale * picked[slots * h:slots * (h + 1)]
        grad_attn = picked[slots * (heads + h):slots * (heads + h + 1)]
        squashed = jnp.tanh(raw / CAP)
        e = jnp.where(live, jnp.exp(CAP * squashed + bias[h]), 0.0)
        attn = e / jnp.sum(e, axis=0, keepdims=True)
        grad = attn * (grad_attn - jnp.sum(attn * grad_attn, axis=0, keepdims=True))
        grad_bias[h] = grad
        grad_raw = scale * grad * (1.0 - squashed * squashed)
        raw_sum, attn_sum = jnp.zeros_like(attn), jnp.zeros_like(attn)
        for t in range(slots):
            same = pos == pos[t:t + 1]
            raw_sum += jnp.where(same, grad_raw[t:t + 1], 0.0)
            attn_sum += jnp.where(same, attn[t:t + 1], 0.0)
        raws.append(raw_sum)
        attns.append(attn_sum)
    spread[...] = jnp.concatenate(raws + attns, axis=0).T
    rims = [go(remote(spread.at[src], xs.at[d], xss.at[d], xsr.at[d], to, chan))
            for d, (to, src) in enumerate(ways)]
    for copy in late[4:]:
        copy.start()

    for b in range(3):
        def write(row, r, x, b=b):
            low = HALO * b + (HALO if b == 2 and r >= HALO else 0)
            p[row, r:r + strip, low:low + HALO] = x
        spread_out(spread, slot_own.at[b], write)

    kinds = LMAX + 1

    def put(kind, h, value):
        low = kind * cl + 16 * h
        g[:, low:low + 16, :] = value.astype(bf16).reshape(M, 16, atoms)

    def weight_terms(kind, low, high):
        for degree in range(kinds):
            ms = range(degree * degree, (degree + 1) * (degree + 1))
            at = slice(kind * cl + low, kind * cl + high)
            acc = nt(jnp.concatenate([g[m, at] for m in ms], axis=1),
                     jnp.concatenate([fx[0, m] for m in ms], axis=1))
            for one in range(low // cl, -(-high // cl)):
                first, last = max(low, one * cl), min(high, one * cl + cl)
                to = ((kind + one) * kinds + degree) * cl
                gw[to + first - one * cl:to + last - one * cl, :] = acc[first - low:last - low]

    def reduce_steps(base, size, near_, red, far, last, sems):
        s1, r1, s2, r2, s3, r3 = sems

        def piece(i):
            return pl.ds(pl.multiple_of(base + i * size, 8), size)

        def one():
            out = [go(remote(gw.at[piece(lax.rem(xy + d, plane))], near_.at[xy], s1.at[d],
                             r1.at[d], beside[d], chan)) for d in range(1, plane)]
            near_[xy] = gw[piece(xy)]
            return out

        def two():
            red[...] = sum(near_[i] for i in range(plane))
            out = [go(remote(red, far.at[z], s2.at[d], r2.at[d], behind[d], chan))
                   for d in range(1, deep)]
            far[z] = red[...]
            return out

        def three():
            last[...] = sum(far[i] for i in range(deep))
            out = [go(remote(last, fin.at[piece(xy)], s3.at[d], r3.at[d], beside[d], chan))
                   for d in range(1, plane)]
            fin[piece(xy)] = last[...]
            return out
        return one, two, three

    def arrive(copies):
        for copy in copies:
            copy.wait_recv()

    a_steps = reduce_steps(0, a_red.shape[0], a_near, a_red, a_far, a_last,
                           (a1s, a1r, a2s, a2r, a3s, a3r))
    b_steps = reduce_steps(2 * kinds * cl, b_red.shape[0], b_near, b_red, b_far, b_last,
                           (b1s, b1r, b2s, b2r, b3s, b3r))
    for h in range(heads):
        mine, rim = head(k, 0, h), head(k, 1, h)
        put(0, h, nt(jnp.concatenate([mine, rim, mine, rim], axis=1),
                     jnp.concatenate([p[h], p[2 * heads + h]], axis=1)))
    for d in range(2):
        rims[d].wait_recv()

        def write(row, r, x, d=d):
            pr[row, HALO * d + r:HALO * d + r + strip, halves[d]] = x
        spread_out(xs.at[d], slot_rim.at[d], write)
    for h in range(heads):
        mine, rim = head(q, 0, h), head(q, 1, h)
        lo = 2 * heads + h
        put(1, h, nn(jnp.concatenate([mine, rim, mine, rim], axis=1),
                     jnp.concatenate([p[h, :, 0:atoms], pr[h], p[lo, :, 0:atoms], pr[lo]], axis=0)))
    weight_terms(0, 0, 2 * cl)
    copies_a = a_steps[0]()
    for h in range(heads):
        mine = head(cx, 0, h)
        hi, lo = heads + h, 3 * heads + h
        inner = nn(jnp.concatenate([mine, mine], axis=1),
                   jnp.concatenate([p[hi, :, 0:atoms], p[lo, :, 0:atoms]], axis=0))
        part[:, 16 * h:16 * h + 16, :] = inner.reshape(M, 16, atoms)
    for h in range(heads):
        arrive(late[2 * h:2 * h + 2])
        rim = head(cx, 1, h)
        hi, lo = heads + h, 3 * heads + h
        outer = nn(jnp.concatenate([rim, rim], axis=1),
                   jnp.concatenate([pr[hi], pr[lo]], axis=0))
        put(2, h, outer + part[:, 16 * h:16 * h + 16, :].reshape(16 * M, atoms))
        if h == heads - 2:
            weight_terms(2, 0, 16 * (heads - 1))
    weight_terms(2, 16 * (heads - 1), cl)
    copies_b = b_steps[0]()
    arrive(copies_a)
    copies_a = a_steps[1]()

    def feature_terms(i):
        for u in range(STEP):
            m = STEP * i + u
            part[m] = nn(wc[math.isqrt(m)], g[m])
        return go(remote(part.at[chunk(i), theirs, :], arrived.at[chunk(i)],
                         ms.at[i], mr.at[i], me, other))

    swap = [feature_terms(i) for i in range(ROUNDS)]
    arrive(copies_b)
    copies_b = b_steps[1]()
    arrive(copies_a)
    copies_a = a_steps[2]()
    for i in range(2):
        swap[i].wait_recv()
    arrive(copies_b)
    copies_b = b_steps[2]()
    outs = []
    for i in range(ROUNDS):
        if i > 1:
            swap[i].wait_recv()
        for u in range(STEP):
            m = STEP * i + u
            gf[m] = (part[m, rows, :] + arrived[m]).astype(bf16)
        outs.append(pltpu.make_async_copy(gf.at[chunk(i)], gf_out.at[chunk(i)], out_sem.at[i]))
        outs[i].start()
    arrive(copies_a)
    split = 2 * kinds * cl
    for n, (copies, at) in enumerate(((copies_a, pl.ds(0, split)),
                                      (copies_b, pl.ds(split, gw_out.shape[0] - split)))):
        if n:
            arrive(copies)
        outs.append(pltpu.make_async_copy(fin.at[at], gw_out.at[at], out_sem.at[ROUNDS + n]))
        outs[-1].start()
    for copy in sent + queue[2 * ROUNDS:]:
        copy.wait_send()
    for copy in outs:
        copy.wait()


def pass_on(*refs):
    n = (len(refs) - 1) // 3
    src, dst, held, sem = refs[:n], refs[n:2 * n], refs[2 * n:3 * n], refs[-1]
    pieces = []
    for a, b, c in zip(src, dst, held):
        cut = a.shape[0] // ROUNDS if a.shape[0] % ROUNDS == 0 else a.shape[0]
        for i in range(0, a.shape[0], cut):
            at = pl.ds(i, cut)
            pieces.append((a.at[at], b.at[at], c.at[at]))
    ins = [pltpu.make_async_copy(a, c, sem.at[0, i]) for i, (a, _, c) in enumerate(pieces)]
    outs = [pltpu.make_async_copy(c, b, sem.at[1, i]) for i, (_, b, c) in enumerate(pieces)]
    for copy in ins:
        copy.start()
    for one, two in zip(ins, outs):
        one.wait()
        two.start()
    for copy in outs:
        copy.wait()


def on_device(features, weights, cotangent, edge_bias, neighbours, valid_mask):
    cl, _, atoms = features.shape
    heads, slots, _ = edge_bias.shape
    feat = jnp.transpose(features, (1, 0, 2))
    cot = jnp.transpose(cotangent, (1, 0, 2))
    w = jnp.transpose(weights, (0, 1, 3, 2))
    S = jax.ShapeDtypeStruct
    both = (2, M, cl, atoms)
    wide = atoms + HALO
    kinds = 3 * (LMAX + 1) * cl
    plane = 16
    deep = lax.axis_size("atom") // plane
    third = (LMAX + 1) * cl
    b_size = -(-third // (8 * plane)) * 8
    V = pltpu.VMEM
    a_row, b_row = (2 * third // plane, 2 * cl), (b_size, 2 * cl)
    padded = (2 * third + plane * b_size, 2 * cl)
    gf, total, grad_bias = pl.pallas_call(
        functools.partial(layer_kernel, plane),
        out_shape=(S((M, cl, atoms), bf16), S((kinds, 2 * cl), f32), S(edge_bias.shape, f32)),
        in_specs=[ANY, ANY, VMEM, VMEM, VMEM, VMEM],
        out_specs=(ANY, ANY, VMEM),
        scratch_shapes=[
            V((2, M, 2 * cl, atoms), bf16), V(both, bf16), V(both, bf16), V(both, bf16),
            V(both, bf16), V((2 * heads, atoms, wide), f32), V((2, slots, HALO), jnp.int32),
            V((atoms, HALO), f32), V((2, HALO, HALO), f32),
            V((3, atoms, HALO), jnp.int32), V((2, HALO, HALO), jnp.int32),
            V((4 * heads, atoms, wide + HALO), bf16), V((4 * heads, atoms, atoms), bf16),
            V((M, 3 * cl, atoms), bf16), V((M, 2 * cl, atoms), f32), V((M, cl, atoms), f32),
            V((M, cl, atoms), bf16), V((LMAX + 1, 2 * cl, 3 * cl), bf16), V(padded, f32),
            V((plane, *a_row), f32), V(a_row, f32), V((deep, *a_row), f32), V(a_row, f32),
            V((plane, *b_row), f32), V(b_row, f32), V((deep, *b_row), f32), V(b_row, f32),
            V(padded, f32),
            DMA((2,)), DMA((ROUNDS + 2,)), DMA((2,)), DMA((2,)), DMA((ROUNDS,)), DMA((ROUNDS,)),
            DMA((2, ROUNDS)), DMA((2, ROUNDS)), DMA((2, ROUNDS)), DMA((2, ROUNDS)),
            DMA((2, heads)), DMA((2, heads)), DMA((2,)), DMA((2,)), DMA((ROUNDS,)), DMA((ROUNDS,)),
            DMA((plane,)), DMA((plane,)), DMA((deep,)), DMA((deep,)), DMA((plane,)), DMA((plane,)),
            DMA((plane,)), DMA((plane,)), DMA((deep,)), DMA((deep,)), DMA((plane,)), DMA((plane,))],
        compiler_params=pltpu.CompilerParams(
            vmem_limit_bytes=62 * 1024 * 1024, collective_id=0, has_side_effects=True),
        name="layer",
    )(feat, cot, w, edge_bias, neighbours, valid_mask)
    results = (gf, total.reshape(3 * (LMAX + 1), cl, 2 * cl), grad_bias)
    gf, total, grad_bias = pl.pallas_call(
        pass_on,
        out_shape=tuple(S(x.shape, x.dtype) for x in results),
        in_specs=[ANY] * 3,
        out_specs=(ANY,) * 3,
        scratch_shapes=[*(V(x.shape, x.dtype) for x in results), DMA((2, 2 * ROUNDS + 1))],
        compiler_params=pltpu.CompilerParams(vmem_limit_bytes=62 * 1024 * 1024),
        name="pass_on",
    )(*results)
    grad_weights = jnp.transpose(total.reshape(3, LMAX + 1, cl, 2 * cl), (0, 1, 3, 2))
    return jnp.transpose(gf, (1, 0, 2)), grad_weights, grad_bias


def solution(mesh):
    return jax.shard_map(
        on_device,
        mesh=mesh,
        in_specs=(P("chan", None, "atom"), P(None, None, None, "chan"), P("chan", None, "atom"),
                  P("chan", None, "atom"), P(None, "atom"), P(None, "atom")),
        out_specs=(P("chan", None, "atom"), P(None, None, None, "chan"), P("chan", None, "atom")),
        check_vma=False,
    )
```

time: 90.4 us -> 85.5 us (0.946)
  the two profiles are of different devices: /device:TPU:8 before, /device:TPU:1 now
where the time goes in v3:
time: 85.5 us; the launch traced here: 84.2 us
  Pallas kernels  83.4 us (98%)
    pallas_call x1, Pallas kernels, on_device(): pl.pallas_call(functools.partial(layer_kernel, plane), out_shape=(S((M, c...  80.6 us
    pallas_call x1, Pallas kernels, on_device(): pl.pallas_call(pass_on, out_shape=tuple((S(x.shape, x.dtype) for x in res...  2.7 us

profile of v3, /device:TPU:1, one launch (start us, length us, event | category | flops | bytes accessed | tf_op | source)
XLA Modules:
  0.0 84.2 jit_solution(1138257151247952386)
XLA Ops:
  0.6 80.6 %layer.1 = (bf16[49,64,256]{2,1,0:T(8,128)(2,1)}, f32[1344,128]{1,0:T(8,128)}, f32[4,16,256]{2,1,0:T(8,128)}) custom-call(bf16[49,64,256]{2,1,0:T(8,128)(2,1)} %bitcast.8, bf16[49,64,256]{2,1,0:T(8,128)(2,1)} %bitcast.9, bf16[3,7,64,128]{3,2,1,0:T(8,128)(2,1)} %bitcast.11, f32[4,16,256]{2,1,0:T(8,128)} %bias.1, s32[16,256]{1,0:T(8,128)} %near.1, s32[16,256]{1,0:T(8,128)} %valid.1), custom_call_target="tpu_custom_call" | custom-call | tf_op jit(solution)/shard_map/layer/pallas_call | solution.py:449
  81.3 2.7 %pass_on.1 = (bf16[49,64,256]{2,1,0:T(8,128)(2,1)}, f32[21,64,128]{2,1,0:T(8,128)}, f32[4,16,256]{2,1,0:T(8,128)}) custom-call(bf16[49,64,256]{2,1,0:T(8,128)(2,1)} %get-tuple-element.9.refs_0_, f32[21,64,128]{2,1,0:T(8,128)} %bitcast.10, f32[4,16,256]{2,1,0:T(8,128)} %get-tuple-element.11.refs_2_), custom_call_target="tpu_custom_call" | custom-call | tf_op jit(solution)/shard_map/pass_on/pallas_call | solution.py:475
